TPU v7x, 128 devices: a whole 4x4x4 slice. The times are simulated.
128 devices in a mesh: rows: 16 (over z_lo, x, core), batch: 8 (over z_hi, y).
Axes of the slice: x: 4, y: 4, z: 4 (z_hi: 2, z_lo: 2; z = z_hi * 2 + z_lo), core: 2. Of those that a mesh axis runs over, the one named last changes fastest.
Arguments:
- bases: bfloat16 [49152, 2048], P('rows', 'batch'), may hold values from -30 to 30
- start: float32 [2048, 512], P('batch'), may hold values from -6 to 6
Outputs:
- modes: bfloat16 [49152, 512], P(('rows', 'batch'))
All inputs are finite; a program needn't handle non-finite values.
Results may differ from a plain program's by a relative error of at most 0.0041.
Values may be sent and summed in bfloat16 or wider, within the bound.
A program may use at most 128 MiB of HBM per device.

v0:
```python
import jax
import jax.numpy as jnp
from jax import lax
from jax.sharding import PartitionSpec as P

ITERS = 2


def inner_cols(left, right):
    return lax.dot_general(
        left, right, (((0,), (0,)), ((), ())), preferred_element_type=jnp.float32
    )


def on_device(bases, start):
    basis_width = bases.shape[1]
    group_count = lax.axis_size("batch")
    all_columns = basis_width * group_count
    energy = lax.psum(jnp.sum(jnp.square(bases.astype(jnp.float32))), ("rows", "batch"))
    diag_mean = energy / all_columns
    partial_value = inner_cols(bases, lax.all_gather(bases, "batch", axis=1, tiled=True))
    gram_rows = lax.psum(partial_value, "rows")
    q_own = start
    for iteration in range(ITERS):
        q_full = lax.all_gather(q_own, "batch", axis=0, tiled=True)
        lifted = jnp.dot(gram_rows, q_full, precision=lax.Precision.HIGHEST) / diag_mean + q_own
        local_correlation = lax.dot_general(
            lifted, lifted, (((0,), (0,)), ((), ())), precision=lax.Precision.HIGHEST
        )
        correlation = lax.psum(local_correlation, "batch")
        factor = jnp.linalg.cholesky(correlation)
        q_own = jax.scipy.linalg.solve_triangular(factor, lifted.T, lower=True).T
    q_low = q_own.astype(jnp.bfloat16)
    modes = lax.psum_scatter(
        jnp.dot(bases, q_low, preferred_element_type=jnp.float32),
        "batch",
        scatter_dimension=0,
        tiled=True,
    )
    return modes.astype(jnp.bfloat16)


def solution(mesh):
    in_specs = (P("rows", "batch"), P("batch", None))
    out_specs = P(("rows", "batch"), None)
    return jax.shard_map(
        on_device, mesh=mesh, in_specs=in_specs, out_specs=out_specs, check_vma=False
    )
```

profile of v0, /device:TPU:1, one launch (start us, length us, event | category | flops | bytes accessed | tf_op | source)
XLA Modules:
  0.0 1044.8 jit_solution(2930456255555356268)
XLA Ops:
  8.1 165.7 %all-gather.4.cloned.1.call-done = bf16[3072,2048]{1,0:T(8,128)(2,1)} async-done(((bf16[3072,256]{1,0:T(8,128)(2,1)}), bf16[3072,2048]{1,0:T(8,128)(2,1)}) %all-gather.4.cloned.1.call-update) | async-done | bytes 12582928 | tf_op jit(solution)/shard_map/all_gather | solution.py:21
  173.8 7.8 fusion.76
  181.7 1.4 multiply_reduce_fusion
  183.1 79.2 %psum.29 = f32[]{:T(128)} all-reduce(f32[]{:T(128)} %multiply_reduce_fusion), channel_id=1, replica_groups=mesh['rows'=16,'batch'=8] {'rows','batch'}, use_global_device_ids=true, to_apply=%region_2.0 | all-reduce | flops 1 | bytes 8 | tf_op jit(solution)/shard_map/psum | solution.py:19
  263.0 108.5 %all-reduce.5.cloned.1.call-done = f32[256,2048]{1,0:T(8,128)} async-done(((f32[256,2048]{1,0:T(8,128)}), f32[256,2048]{1,0:T(8,128)}) %all-reduce.5.cloned.1.call-update) | async-done | bytes 2097168 | tf_op jit(solution)/shard_map/psum | solution.py:22
  371.4 6.2 fusion
  377.7 2.1 fusion.77
  380.0 83.4 %all-reduce.7.cloned.1.call-done = f32[512,512]{0,1:T(8,128)} async-done(((f32[512,512]{0,1:T(8,128)}), f32[512,512]{0,1:T(8,128)}) %all-reduce.7.cloned.1.call-update) | async-done | bytes 1048592 | tf_op jit(solution)/shard_map/psum | solution.py:30
  463.4 2.7 copy.4
  466.1 1.4 fusion.2
  467.6 1.0 copy-done.4
  468.6 11.7 %cholesky.286 = f32[128,128]{1,0:T(8,128)S(1)} custom-call(f32[128,128]{1,0:T(8,128)S(1)} %cholesky.426), custom_call_target="Cholesky" | custom-call | tf_op jit(solution)/shard_map/jit(cholesky)/cholesky | solution.py:31
  480.3 9.8 custom-call.27
  490.3 1.2 constant_dynamic-update-slice_fusion.5
  491.5 1.3 convolution_subtract_fusion.1
  492.8 11.7 %cholesky.305 = f32[128,128]{1,0:T(8,128)S(1)} custom-call(f32[128,128]{1,0:T(8,128)S(1)} %cholesky.430), custom_call_target="Cholesky" | custom-call | tf_op jit(solution)/shard_map/jit(cholesky)/cholesky | solution.py:31
  504.5 10.0 custom-call.28
  514.8 1.3 convolution_subtract_fusion.7
  516.1 11.7 %cholesky.326 = f32[128,128]{1,0:T(8,128)S(1)} custom-call(f32[128,128]{1,0:T(8,128)S(1)} %cholesky.435), custom_call_target="Cholesky" | custom-call | tf_op jit(solution)/shard_map/jit(cholesky)/cholesky | solution.py:31
  528.6 9.8 custom-call.29
  538.6 1.2 convolution_subtract_fusion.11
  539.8 11.7 %cholesky.343 = f32[128,128]{1,0:T(8,128)S(1)} custom-call(f32[128,128]{1,0:T(8,128)S(1)} %convolution_subtract_fusion.11), custom_call_target="Cholesky" | custom-call | tf_op jit(solution)/shard_map/jit(cholesky)/cholesky | solution.py:31
  555.4 1.5 select_select_fusion.1
  557.0 11.7 %while.4 = (s32[]{:T(128)}, f32[512,512]{1,0:T(8,128)}, s32[4,2]{0,1:T(2,128)S(1)}, f32[4,128,128]{2,1,0:T(8,128)S(1)}, s32[]{:T(128)}) while((s32[]{:T(128)}, f32[512,512]{1,0:T(8,128)}, s32[4,2]{0,1:T(2,128)S(1)}, f32[4,128,128]{2,1,0:T(8,128)S(1)}, s32[]{:T(128)}) %tuple.52), condition=%wide.while_cond, body=%wide.while_body.sunk | while | flops 2 | bytes 131181 | solution.py:32
  557.6 2.3 bitcast_dynamic-update-slice_fusion.4
  560.6 2.3 bitcast_dynamic-update-slice_fusion.4
  563.5 2.3 bitcast_dynamic-update-slice_fusion.4
  566.5 2.2 bitcast_dynamic-update-slice_fusion.4
  568.7 39.3 %custom-call.30 = f32[4,128,128]{1,2,0:T(8,128)S(1)} custom-call(f32[4,128,128]{2,1,0:T(8,128)S(1)} %get-tuple-element.21), custom_call_target="InvertDiagBlocksLowerTriangular" | custom-call | tf_op jit(solution)/shard_map/jit(_solve_triangular)/triangular_solve | solution.py:32
  608.3 1.2 convolution_subtract_fusion.9
  609.9 1.5 convolution_subtract_fusion.6
  611.7 1.7 convolution_subtract_fusion.5
  614.9 74.7 %all-gather.8.cloned.1.call-done = f32[2048,512]{1,0:T(8,128)} async-done(((f32[256,512]{1,0:T(8,128)}), f32[2048,512]{1,0:T(8,128)}) %all-gather.8.cloned.1.call-update) | async-done | bytes 4194320 | tf_op jit(solution)/shard_map/all_gather | solution.py:25
  689.6 6.3 bitcast_add_fusion.2
  695.9 2.1 fusion.3
  698.3 80.6 %all-reduce.9.cloned.1.call-done = f32[512,512]{0,1:T(8,128)} async-done(((f32[512,512]{0,1:T(8,128)}), f32[512,512]{0,1:T(8,128)}) %all-reduce.9.cloned.1.call-update) | async-done | bytes 1048592 | tf_op jit(solution)/shard_map/psum | solution.py:30
  778.9 2.7 copy.10
  781.6 1.4 fusion.1
  783.1 1.0 copy-done.3
  784.1 11.7 %cholesky.358 = f32[128,128]{1,0:T(8,128)S(1)} custom-call(f32[128,128]{1,0:T(8,128)S(1)} %cholesky.439), custom_call_target="Cholesky" | custom-call | tf_op jit(solution)/shard_map/jit(cholesky)/cholesky | solution.py:31
  796.0 9.8 custom-call.31
  805.8 1.2 constant_dynamic-update-slice_fusion.3
  807.0 1.3 convolution_subtract_fusion
  808.3 11.7 %cholesky.377 = f32[128,128]{1,0:T(8,128)S(1)} custom-call(f32[128,128]{1,0:T(8,128)S(1)} %cholesky.443), custom_call_target="Cholesky" | custom-call | tf_op jit(solution)/shard_map/jit(cholesky)/cholesky | solution.py:31
  821.4 10.0 custom-call.32
  831.7 1.3 convolution_subtract_fusion.4
  833.0 11.7 %cholesky.398 = f32[128,128]{1,0:T(8,128)S(1)} custom-call(f32[128,128]{1,0:T(8,128)S(1)} %cholesky.448), custom_call_target="Cholesky" | custom-call | tf_op jit(solution)/shard_map/jit(cholesky)/cholesky | solution.py:31
  845.4 9.8 custom-call.33
  855.4 1.2 convolution_subtract_fusion.10
  856.6 11.7 %cholesky.415 = f32[128,128]{1,0:T(8,128)S(1)} custom-call(f32[128,128]{1,0:T(8,128)S(1)} %convolution_subtract_fusion.10), custom_call_target="Cholesky" | custom-call | tf_op jit(solution)/shard_map/jit(cholesky)/cholesky | solution.py:31
  871.7 1.4 select_select_fusion
  873.0 11.7 %while.5 = (s32[]{:T(128)}, f32[512,512]{1,0:T(8,128)}, s32[4,2]{0,1:T(2,128)S(1)}, f32[4,128,128]{2,1,0:T(8,128)S(1)}, s32[]{:T(128)}) while((s32[]{:T(128)}, f32[512,512]{1,0:T(8,128)}, s32[4,2]{0,1:T(2,128)S(1)}, f32[4,128,128]{2,1,0:T(8,128)S(1)}, s32[]{:T(128)}) %tuple.72), condition=%wide.while_cond.clone, body=%wide.while_body.clone.sunk | while | flops 2 | bytes 131181 | solution.py:32
  873.7 2.3 bitcast_dynamic-update-slice_fusion.5
  876.7 2.3 bitcast_dynamic-update-slice_fusion.5
  879.6 2.3 bitcast_dynamic-update-slice_fusion.5
  882.6 2.2 bitcast_dynamic-update-slice_fusion.5
  884.8 39.3 %custom-call.34 = f32[4,128,128]{1,2,0:T(8,128)S(1)} custom-call(f32[4,128,128]{2,1,0:T(8,128)S(1)} %get-tuple-element.22), custom_call_target="InvertDiagBlocksLowerTriangular" | custom-call | tf_op jit(solution)/shard_map/jit(_solve_triangular)/triangular_solve | solution.py:32
  924.4 1.2 convolution_subtract_fusion.8
  926.0 1.5 convolution_subtract_fusion.3
  927.8 1.8 convolution_subtract_fusion.2
  929.9 3.7 convolution_bitcast_fusion
  933.6 101.8 %reduce-scatter.2.cloned.1.call-done = f32[384,512]{0,1:T(8,128)} async-done(((f32[3072,512]{0,1:T(8,128)}), f32[384,512]{0,1:T(8,128)}) %reduce-scatter.2.cloned.1.call-update) | async-done | bytes 786448 | tf_op jit(solution)/shard_map/reduce_scatter | solution.py:34
  1035.4 1.2 convert_element_type.12
  1036.6 0.9 copy.11
  (84 shorter events, 17.4 us)
Async XLA Ops:
  6.5 167.2 %copy-start = (bf16[3072,256]{1,0:T(8,128)(2,1)S(1)}, bf16[3072,256]{1,0:T(8,128)(2,1)}, u32[]{:S(2)}) copy-start(bf16[3072,256]{1,0:T(8,128)(2,1)} %param.5) | copy-start | bytes 4718596
  6.5 167.2 %all-gather.4.cloned.1.call-start = ((), (), s32[]{:S(2)}) async-start(), calls=%async_computation.1 | async-start | bytes 14155776 | tf_op jit(solution)/shard_map/all_gather | solution.py:21
  7.3 255.7 %all-gather.6.cloned.1.call-start = ((), (), s32[]{:S(2)}) async-start(), calls=%async_computation.3 | async-start | bytes 4718592 | tf_op jit(solution)/shard_map/all_gather | solution.py:25
  8.0 363.4 %all-reduce.5.cloned.1.call-start = ((), (), s32[]{:S(2)}) async-start(), calls=%async_computation.2 | async-start | bytes 4194304 | tf_op jit(solution)/shard_map/psum | solution.py:22
  181.6 189.9 %copy-start.5 = (f32[256,512]{1,0:T(8,128)S(1)}, f32[256,512]{1,0:T(8,128)}, u32[]{:S(2)}) copy-start(f32[256,512]{1,0:T(8,128)} %param.6) | copy-start | bytes 1572868
  181.6 281.8 %all-reduce.7.cloned.1.call-start = ((), (), s32[]{:S(2)}) async-start(), calls=%async_computation.4 | async-start | bytes 2097152 | tf_op jit(solution)/shard_map/psum | solution.py:30
  379.8 309.9 %all-gather.8.cloned.1.call-start = ((), (), s32[]{:S(2)}) async-start(), calls=%async_computation.5 | async-start | bytes 4718592 | tf_op jit(solution)/shard_map/all_gather | solution.py:25
  463.4 2.7 copy-start.1
  467.6 1.0 copy-start.4
  614.9 164.1 %all-reduce.9.cloned.1.call-start = ((), (), s32[]{:S(2)}) async-start(), calls=%async_computation.6 | async-start | bytes 2097152 | tf_op jit(solution)/shard_map/psum | solution.py:30
  698.1 337.3 %reduce-scatter.2.cloned.1.call-start = ((), (), s32[]{:S(2)}) async-start(), calls=%async_computation.7 | async-start | bytes 7077888 | tf_op jit(solution)/shard_map/reduce_scatter | solution.py:34
  778.9 2.7 copy-start.2
  783.1 1.0 copy-start.3
Sparse Core Ops, SparseCore 0:
  9.5 164.1 all-gather.3
  176.1 71.4 all-gather.5
  250.1 121.2 all-reduce.4
  379.9 83.4 all-reduce.6
  615.0 74.6 all-gather.7
  698.2 80.6 all-reduce.8
  933.7 101.6 reduce-scatter.1
where the time goes:
time: 1050 us; the launch traced here: 1040 us
  waiting for transfers between devices  616 us (59%)
  other arithmetic  246 us (23%)
  blocking collectives  79.2 us (8%)
  matrix products  50.5 us (5%)
  local copies, waits for them, and re-layouts  32.1 us (3%)
  between operations  20.1 us (2%)
    all_gather x1, waiting for transfers between devices, on_device(): lax.all_gather(bases, 'batch', axis=1, tiled=True)  166 us
    psum x2, waiting for transfers between devices, on_device(): correlation = lax.psum(local_correlation, 'batch')  164 us
    another operation x29, other arithmetic, on_device(): factor = jnp.linalg.cholesky(correlation)  158 us
    psum x1, waiting for transfers between devices, on_device(): gram_rows = lax.psum(partial_value, 'rows')  108 us
    reduce_scatter x1, waiting for transfers between devices, on_device(): lax.psum_scatter(jnp.dot(bases, q_low, preferred_element_type=jnp.float32...  102 us
    another operation x5, other arithmetic, on_device(): q_own = jax.scipy.linalg.solve_triangular(factor, lifted.T, lower=True).T  81.5 us
    psum x1, blocking collectives, on_device(): lax.psum(jnp.sum(jnp.square(bases.astype(jnp.float32))), ('rows', 'batch'))  79.2 us
    all_gather x2, waiting for transfers between devices, on_device(): q_full = lax.all_gather(q_own, 'batch', axis=0, tiled=True)  74.8 us
  transfers between devices with their start and end apart: 7, of which 6 were waited for; matrix products, arithmetic and copies ran while one was open for 1% of the time, Pallas kernels for 0%

commit v1 on v0

v1 whole, which is shorter than its diff:
```python
import functools

import jax
import jax.numpy as jnp
from jax import lax
from jax.experimental import pallas as pl
from jax.experimental.pallas import tpu as pltpu
from jax.sharding import PartitionSpec as P

ITERS = 2
NB = 128
HIGHEST = lax.Precision.HIGHEST
VMEM_SPEC = pl.BlockSpec(memory_space=pltpu.VMEM)


def dot_f32(left, right, left_dim, right_dim):
    return lax.dot_general(
        left, right, (((left_dim,), (right_dim,)), ((), ())),
        precision=HIGHEST, preferred_element_type=jnp.float32,
    )


def dot_low(left, right, left_dim, right_dim):
    return lax.dot_general(
        left, right, (((left_dim,), (right_dim,)), ((), ())),
        preferred_element_type=jnp.float32,
    )


def split(value):
    high = value.astype(jnp.bfloat16)
    return high, (value - high.astype(jnp.float32)).astype(jnp.bfloat16)


def factor_block(aug, work):
    row = lax.broadcasted_iota(jnp.int32, (8, NB), 0)
    for panel in range(NB // 8):
        low = 8 * panel
        left = aug[low:low + 8, :NB]
        right = aug[low:low + 8, NB:]
        cols = [jnp.broadcast_to(left[:, low + j:low + j + 1], (8, NB)) for j in range(8)]
        pivots = jnp.zeros((8, NB), jnp.float32)
        for k in range(8):
            pivot = jnp.broadcast_to(cols[k][k:k + 1, :], (8, NB))
            mult = jnp.where(row > k, cols[k] / pivot, 0.0)
            pivots = jnp.where(row == k, pivot, pivots)
            for j in range(k + 1, 8):
                cols[j] = cols[j] - mult * jnp.broadcast_to(cols[j][k:k + 1, :], (8, NB))
            left = left - mult * jnp.broadcast_to(left[k:k + 1, :], (8, NB))
            right = right - mult * jnp.broadcast_to(right[k:k + 1, :], (8, NB))
        scale = lax.rsqrt(pivots)
        rows = jnp.concatenate([left * scale, right * scale], axis=1)
        work[low:low + 8, :] = rows
        if low + 8 < NB:
            aug[low + 8:, :] = aug[low + 8:, :] - dot_f32(rows[:, :NB], rows, 0, 0)[low + 8:, :]


def factor_kernel(n, c_ref, t_ref, rest, upper, aug, work, inverses):
    blocks = n // NB
    rest[...] = c_ref[...]
    t_ref[...] = jnp.zeros_like(t_ref)
    row = lax.broadcasted_iota(jnp.int32, (NB, NB), 0)
    col = lax.broadcasted_iota(jnp.int32, (NB, NB), 1)

    @pl.loop(0, blocks)
    def _(j):
        here = pl.ds(pl.multiple_of(j * NB, NB), NB)
        aug[:, :NB] = rest[here, here]
        aug[:, NB:] = jnp.where(row == col, 1.0, 0.0)
        factor_block(aug, work)
        inverse = jnp.where(row >= col, work[:, NB:], 0.0)
        inverses[j] = inverse
        rows = dot_f32(inverse, rest[here, :], 1, 0)
        upper[here, :] = rows

        @pl.when(j < blocks - 1)
        def _():
            rest[...] = rest[...] - dot_f32(rows, rows, 0, 0)

    for j in range(blocks):
        here = slice(j * NB, (j + 1) * NB)
        block = inverses[j].T
        t_ref[here, here] = block
        if j:
            above = slice(0, j * NB)
            t_ref[above, here] = -dot_f32(
                t_ref[above, above], dot_f32(upper[above, here], block, 1, 0), 1, 0
            )


def inverse_factor(correlation):
    n = correlation.shape[0]
    return pl.pallas_call(
        functools.partial(factor_kernel, n),
        out_shape=jax.ShapeDtypeStruct((n, n), jnp.float32),
        in_specs=[VMEM_SPEC],
        out_specs=VMEM_SPEC,
        scratch_shapes=[
            pltpu.VMEM((n, n), jnp.float32),
            pltpu.VMEM((n, n), jnp.float32),
            pltpu.VMEM((NB, 2 * NB), jnp.float32),
            pltpu.VMEM((NB, 2 * NB), jnp.float32),
            pltpu.VMEM((n // NB, NB, NB), jnp.float32),
        ],
    )(correlation)


def gram_kernel(a_ref, q_ref, out_ref):
    a = a_ref[...]
    high, low = split(q_ref[...])
    inner = dot_low(a, high, 1, 0) + dot_low(a, low, 1, 0)
    high, low = split(inner)
    out_ref[...] = dot_low(a, high, 0, 0) + dot_low(a, low, 0, 0)


def gram_apply(a, q):
    return pl.pallas_call(
        gram_kernel,
        out_shape=jax.ShapeDtypeStruct(q.shape, jnp.float32),
        in_specs=[VMEM_SPEC, VMEM_SPEC],
        out_specs=VMEM_SPEC,
    )(a, q)


def on_device(bases, start):
    basis_width = bases.shape[1]
    all_columns = basis_width * lax.axis_size("batch")
    own_rows = lax.all_to_all(bases, "batch", split_axis=0, concat_axis=1, tiled=True)
    energy = lax.psum(jnp.sum(jnp.square(own_rows.astype(jnp.float32))), ("rows", "batch"))
    diag_mean = energy / all_columns
    q = lax.all_gather(start, "batch", axis=0, tiled=True)
    for iteration in range(ITERS):
        lifted = lax.psum(gram_apply(own_rows, q), ("rows", "batch")) / diag_mean + q
        correlation = dot_f32(lifted, lifted, 0, 0)
        q = dot_f32(lifted, inverse_factor(correlation), 1, 0)
    q_low = q.astype(jnp.bfloat16)
    return jnp.dot(own_rows, q_low, preferred_element_type=jnp.float32).astype(jnp.bfloat16)


def solution(mesh):
    in_specs = (P("rows", "batch"), P("batch", None))
    out_specs = P(("rows", "batch"), None)
    return jax.shard_map(
        on_device, mesh=mesh, in_specs=in_specs, out_specs=out_specs, check_vma=False
    )
```

time: 1050 us -> 572 us (0.54)
  waiting for transfers between devices: 616 us -> 288 us
  other arithmetic: 246 us -> 1.41 us
  Pallas kernels: 0 us -> 102 us
  local copies, waits for them, and re-layouts: 32.1 us -> 2.34 us
  blocking collectives: 79.2 us -> 99.4 us
    another operation x34 -> x0, other arithmetic: 239 us -> none  [the longest x29 158 us: on_device(): factor = jnp.linalg.cholesky(correlation)]
    all_gather x3 -> x1, waiting for transfers between devices: 240 us -> 48.5 us  [on_device(): q = lax.all_gather(start, 'batch', axis=0, tiled=True)]
    pallas_call x0 -> x4, Pallas kernels: none -> 102 us  [the longest x2 84.7 us: inverse_factor(): pl.pallas_call(functools.partial(factor_kernel, n), out_shape=jax.ShapeDt...]
    reduce_scatter x1 -> x0, waiting for transfers between devices: 102 us -> none  [on_device(): lax.psum_scatter(jnp.dot(bases, q_low, preferred_element_type=jnp.float32...]
    psum x3 -> x2, waiting for transfers between devices: 272 us -> 238 us  [on_device(): lax.psum(gram_apply(own_rows, q), ('rows', 'batch')) / diag_mean + q]
    all_to_all x0 -> x1, blocking collectives: none -> 34.1 us  [on_device(): lax.all_to_all(bases, 'batch', split_axis=0, concat_axis=1, tiled=True)]
    dot_general x6 -> x5, matrix products: 28.2 us -> 60.3 us  [the longest x4 59 us: dot_f32(): lax.dot_general(left, right, (((left_dim,), (right_dim,)), ((), ())), pre...]
    another operation x38 -> x0, local copies, waits for them, and re-layouts: 23.8 us -> none  [the longest x30 23.6 us: on_device(): q_own = jax.scipy.linalg.solve_triangular(factor, lifted.T, lower=True).T]
  transfers between devices with their start and end apart: 7 -> 3, of which waited for: 6 -> 3; matrix products, arithmetic and copies ran while one was open for 1% -> 0% of each run, Pallas kernels for 0% -> 0%
where the time goes in v1:
time: 572 us; the launch traced here: 567 us
  waiting for transfers between devices  288 us (50%)
  Pallas kernels  102 us (18%)
  blocking collectives  99.4 us (17%)
  matrix products  60.3 us (11%)
  between operations  14.1 us (2%)
    psum x2, waiting for transfers between devices, on_device(): lax.psum(gram_apply(own_rows, q), ('rows', 'batch')) / diag_mean + q  238 us
    pallas_call x2, Pallas kernels, inverse_factor(): pl.pallas_call(functools.partial(factor_kernel, n), out_shape=jax.ShapeDt...  84.7 us
    psum x1, blocking collectives, on_device(): lax.psum(jnp.sum(jnp.square(own_rows.astype(jnp.float32))), ('rows', 'bat...  65.3 us
    dot_general x4, matrix products, dot_f32(): lax.dot_general(left, right, (((left_dim,), (right_dim,)), ((), ())), pre...  59 us
    all_gather x1, waiting for transfers between devices, on_device(): q = lax.all_gather(start, 'batch', axis=0, tiled=True)  48.5 us
    all_to_all x1, blocking collectives, on_device(): lax.all_to_all(bases, 'batch', split_axis=0, concat_axis=1, tiled=True)  34.1 us
    pallas_call x2, Pallas kernels, gram_apply(): pl.pallas_call(gram_kernel, out_shape=jax.ShapeDtypeStruct(q.shape, jnp.f...  17.4 us
  transfers between devices with their start and end apart: 3, of which 3 were waited for; matrix products, arithmetic and copies ran while one was open for 0% of the time, Pallas kernels for 0%

profile of v1, /device:TPU:1, one launch (start us, length us, event | category | flops | bytes accessed | tf_op | source)
XLA Modules:
  0.0 567.4 jit_solution(14945087297818870707)
XLA Ops:
  6.5 0.0 all-gather.2.cloned.1.call-start
  6.5 0.7 all-gather.2.cloned.1.call-update
  7.3 0.0 all-reduce.3.cloned.1.call-start
  7.3 34.1 %all_to_all.19 = bf16[8,384,256]{2,1,0:T(8,128)(2,1)S(1)} all-to-all(bf16[8,384,256]{2,1,0:T(8,128)(2,1)} %bitcast.15), channel_id=1, replica_groups=mesh['rows'=16,'batch'=8] {'batch'}, dimensions={0} | all-to-all | bytes 3145728 | tf_op jit(solution)/shard_map/all_to_all | solution.py:128
  41.4 1.4 copy.7
  42.8 48.5 %all-gather.2.cloned.1.call-done.q_ref = f32[2048,512]{1,0:T(8,128)} async-done(((f32[256,512]{1,0:T(8,128)}), f32[2048,512]{1,0:T(8,128)}) %all-gather.2.cloned.1.call-update) | async-done | bytes 4194320 | tf_op jit(solution)/shard_map/all_gather | solution.py:131
  91.3 8.7 %shard_map.28 = f32[2048,512]{1,0:T(8,128)} custom-call(bf16[384,2048]{1,0:T(8,128)(2,1)} %bitcast.11, f32[2048,512]{1,0:T(8,128)} %all-gather.2.cloned.1.call-done.q_ref), custom_call_target="tpu_custom_call" | custom-call | tf_op jit(solution)/shard_map/pallas_call | solution.py:117
  99.9 0.0 all-reduce.3.cloned.1.call-update
  100.0 0.0 all-reduce.5.cloned.1.call-start
  100.0 1.4 multiply_reduce_fusion
  101.4 65.3 %psum.22 = f32[]{:T(128)} all-reduce(f32[]{:T(128)} %multiply_reduce_fusion), channel_id=1, replica_groups=mesh['rows'=16,'batch'=8] {'rows','batch'}, use_global_device_ids=true, to_apply=%region_2.0 | all-reduce | flops 1 | bytes 8 | tf_op jit(solution)/shard_map/psum | solution.py:129
  167.4 85.5 %all-reduce.3.cloned.1.call-done = f32[2048,512]{1,0:T(8,128)} async-done(((f32[2048,512]{1,0:T(8,128)}), f32[2048,512]{1,0:T(8,128)}) %all-reduce.3.cloned.1.call-update) | async-done | bytes 4194320 | tf_op jit(solution)/shard_map/psum | solution.py:133
  253.0 19.2 %fusion.2.c_ref = f32[512,512]{1,0:T(8,128)} fusion(f32[2048,512]{1,0:T(8,128)} %all-gather.2.cloned.1.call-done.q_ref, f32[2048,512]{1,0:T(8,128)} %all-reduce.3.cloned.1.call-done, f32[]{:T(128)S(6)} %div.13), kind=kOutput, calls=%fused_computation.7 | convolution fusion | flops 6444548096 | bytes 9437188 | tf_op jit(solution)/shard_map/dot_general | solution.py:17
  272.1 42.3 %shard_map.29 = f32[512,512]{1,0:T(8,128)} custom-call(f32[512,512]{1,0:T(8,128)} %fusion.2.c_ref), custom_call_target="tpu_custom_call" | custom-call | tf_op jit(solution)/shard_map/pallas_call | solution.py:93
  314.4 11.0 %fusion.1.q_ref = f32[2048,512]{1,0:T(8,128)} fusion(f32[512,512]{1,0:T(8,128)} %shard_map.29, f32[2048,512]{1,0:T(8,128)} %all-gather.2.cloned.1.call-done.q_ref, f32[2048,512]{1,0:T(8,128)} %all-reduce.3.cloned.1.call-done, f32[]{:T(128)S(6)} %div.13), kind=kOutput, calls=%fused_computation.6 | convolution fusion | flops 6444548096 | bytes 13631492 | tf_op jit(solution)/shard_map/dot_general | solution.py:17
  325.4 8.7 %shard_map.30 = f32[2048,512]{1,0:T(8,128)} custom-call(bf16[384,2048]{1,0:T(8,128)(2,1)} %bitcast.12, f32[2048,512]{1,0:T(8,128)} %fusion.1.q_ref), custom_call_target="tpu_custom_call" | custom-call | tf_op jit(solution)/shard_map/pallas_call | solution.py:117
  334.2 0.0 all-reduce.5.cloned.1.call-update
  334.2 152.8 %all-reduce.5.cloned.1.call-done = f32[2048,512]{1,0:T(8,128)} async-done(((f32[2048,512]{1,0:T(8,128)}), f32[2048,512]{1,0:T(8,128)}) %all-reduce.5.cloned.1.call-update) | async-done | bytes 4194320 | tf_op jit(solution)/shard_map/psum | solution.py:133
  487.0 19.1 %fusion.3.c_ref = f32[512,512]{1,0:T(8,128)} fusion(f32[2048,512]{1,0:T(8,128)} %fusion.1.q_ref, f32[2048,512]{1,0:T(8,128)} %all-reduce.5.cloned.1.call-done, f32[]{:T(128)S(6)} %div.13), kind=kOutput, calls=%fused_computation.8 | convolution fusion | flops 6444548096 | bytes 9437188 | tf_op jit(solution)/shard_map/dot_general | solution.py:17
  506.2 42.5 %shard_map.31 = f32[512,512]{1,0:T(8,128)} custom-call(f32[512,512]{1,0:T(8,128)} %fusion.3.c_ref), custom_call_target="tpu_custom_call" | custom-call | tf_op jit(solution)/shard_map/pallas_call | solution.py:93
  548.6 0.0 copy-start
  548.6 9.7 %convolution_convert_fusion = bf16[2048,512]{1,0:T(8,128)(2,1)S(1)} fusion(f32[512,512]{1,0:T(8,128)} %shard_map.31, f32[2048,512]{1,0:T(8,128)} %fusion.1.q_ref, f32[2048,512]{1,0:T(8,128)} %all-reduce.5.cloned.1.call-done, f32[]{:T(128)S(6)} %div.13), kind=kOutput, calls=%fused_computation.3 | convolution fusion | flops 6445596672 | bytes 11534340 | tf_op jit(solution)/shard_map/dot_general | solution.py:17
  558.3 0.0 copy-done
  558.3 1.3 fusion
  559.6 0.9 copy.6
Async XLA Ops:
  6.5 84.7 %all-gather.2.cloned.1.call-start = ((), (), s32[]{:S(2)}) async-start(), calls=%async_computation.1 | async-start | bytes 4718592 | tf_op jit(solution)/shard_map/all_gather | solution.py:131
  7.3 245.7 %all-reduce.3.cloned.1.call-start = ((), (), s32[]{:S(2)}) async-start(), calls=%async_computation.2 | async-start | bytes 8388608 | tf_op jit(solution)/shard_map/psum | solution.py:133
  100.0 387.1 %all-reduce.5.cloned.1.call-start = ((), (), s32[]{:S(2)}) async-start(), calls=%async_computation.3 | async-start | bytes 8388608 | tf_op jit(solution)/shard_map/psum | solution.py:133
  548.6 9.7 %copy-start = (bf16[8,48,8,256]{3,2,0,1:T(8,128)(2,1)S(1)}, bf16[8,48,8,256]{3,2,0,1:T(8,128)(2,1)}, u32[]{:S(2)}) copy-start(bf16[8,48,8,256]{3,2,0,1:T(8,128)(2,1)} %copy.7) | copy-start | bytes 4718596
Sparse Core Ops, SparseCore 0:
  9.7 81.5 all-gather.1
  100.1 152.8 all-reduce.2
  334.3 152.6 all-reduce.4

commit v2 on v0

v2 whole, which is shorter than its diff:
```python
import functools

import jax
import jax.numpy as jnp
from jax import lax
from jax.experimental import pallas as pl
from jax.experimental.pallas import tpu as pltpu
from jax.sharding import PartitionSpec as P

NB = 128
GROUPS = 8
RING = 4
CHIPS = 64
ORDERS = (("x", "y", "z"), ("y", "z", "x"), ("z", "x", "y"))
UNITS = (24, 24, 16)
HIGHEST = lax.Precision.HIGHEST
VMEM_SPEC = pl.BlockSpec(memory_space=pltpu.VMEM)
F32, BF16 = jnp.float32, jnp.bfloat16
NN, NT, TN = ((1,), (0,)), ((1,), (1,)), ((0,), (0,))


def dot_f32(left, right, dims):
    return lax.dot_general(
        left, right, (dims, ((), ())), precision=HIGHEST, preferred_element_type=F32
    )


def dot_low(left, right, dims):
    return lax.dot_general(left, right, (dims, ((), ())), preferred_element_type=F32)


def split(value):
    high = value.astype(BF16)
    return high, (value - high.astype(F32)).astype(BF16)


def stack(value):
    return jnp.concatenate(split(value), axis=0)


def fold(value):
    half = value.shape[0] // 2
    return value[:half] + value[half:]


def span(start, size, unit):
    return pl.ds(pl.multiple_of(start, unit), size)


def position():
    rows, batch = lax.axis_index("rows"), lax.axis_index("batch")
    return {
        "x": rows // 2 % 4,
        "y": batch % 4,
        "z": batch // 4 * 2 + rows // 8,
        "core": rows % 2,
    }


def device_at(pos):
    return {
        "rows": pos["z"] % 2 * 8 + pos["x"] * 2 + pos["core"],
        "batch": pos["z"] // 2 * 4 + pos["y"],
    }


def ring_peer(pos, axis, distance):
    there = dict(pos)
    there[axis] = (pos[axis] + distance) % RING
    return there


def sibling(pos):
    there = dict(pos)
    there["core"] = 1 - pos["core"]
    return there


def greet(peers):
    barrier = pltpu.get_barrier_semaphore()
    for peer in peers:
        pl.semaphore_signal(
            barrier, inc=1, device_id=device_at(peer), device_id_type=pl.DeviceIdType.MESH
        )
    pl.semaphore_wait(barrier, len(peers))


class Copies:
    def __init__(self, send_sem, recv_sem):
        self.send_sem, self.recv_sem = send_sem, recv_sem

    def copy(self, index, src, dst, peer):
        return pltpu.make_async_remote_copy(
            src_ref=src, dst_ref=dst,
            send_sem=self.send_sem.at[index], recv_sem=self.recv_sem.at[index],
            device_id=device_at(peer), device_id_type=pl.DeviceIdType.MESH,
        )


def batch_partners(pos, batch, count):
    partners = []
    for distance in range(1, count):
        other = (batch + distance) % count
        there = dict(pos)
        there["y"] = other % 4
        there["z"] = other // 4 * 2 + pos["z"] % 2
        partners.append(there)
    return partners


def exchange(
    pos, bases_ref, turned, a_ref, q_ref, energy_ref, e_send, e_recv, copies, own_sem
):
    core, x = pos["core"], pos["x"]
    batch = lax.axis_index("batch")
    count = lax.axis_size("batch")
    height = bases_ref.shape[0] // count
    width = bases_ref.shape[1]
    quarter = 64
    partners = batch_partners(pos, batch, count)
    x_peers = [ring_peer(pos, "x", d) for d in (1, 2, 3)]
    made = []

    def start(src, dst, peer):
        copy = copies.copy(len(made), src, dst, peer)
        copy.start()
        made.append(copy)
        return copy

    own_rows = span(core * height, height, 16)
    mine = span(x * quarter, quarter, 8)
    turned_rows = span(core * 256 + x * quarter, quarter, 8)

    def columns(which):
        return span(which * width, width, 128)

    def block_rows(which):
        return span(which * height, height, 16)

    def piece(which, half):
        return q_ref.at[which * 2 + half, mine, :]

    own_start = []
    for half in range(2):
        own = pltpu.make_async_copy(
            turned.at[turned_rows, half * 128:(half + 1) * 128], piece(batch, half),
            own_sem.at[half],
        )
        own.start()
        own_start.append(own)
    start_in = [
        [start(turned.at[turned_rows, half * 128:(half + 1) * 128], piece(batch, half), there)
         for half in range(2)]
        for there in partners
    ]
    x_in = [
        start(turned.at[turned_rows, half * 128:(half + 1) * 128], piece(batch, half), there)
        for half in range(2) for there in x_peers
    ]
    block_in = [
        start(bases_ref.at[block_rows((batch + d) % count), :],
              a_ref.at[own_rows, columns(batch)], there)
        for d, there in enumerate(partners, 1)
    ]
    own_block = pltpu.make_async_copy(
        bases_ref.at[block_rows(batch), :], a_ref.at[own_rows, columns(batch)], own_sem.at[2]
    )
    own_block.start()
    aside = [
        start(bases_ref.at[block_rows(batch), :], a_ref.at[own_rows, columns(batch)],
              sibling(pos))
    ]

    def add_square(step, total):
        value = bases_ref[span(step * 64, 64, 64), :].astype(F32)
        value = value * value
        return total + jnp.sum(value.reshape(8, 8, 2 * 128), axis=0)

    total = lax.fori_loop(
        0, bases_ref.shape[0] // 64, add_square, jnp.zeros((8, 2 * 128), F32)
    )
    total = total[:, :128] + total[:, 128:]

    for distance, pair in enumerate(start_in, 1):
        for copy in pair:
            copy.wait_recv()
        other = (batch + count - distance) % count
        block = q_ref.at[span(other * 2, 2, 2), mine, :]
        x_in += [start(block, block, there) for there in x_peers]
    for copy in own_start:
        copy.wait()
    rings = [[ring_peer(pos, axis, d) for d in (1, 2, 3)] for axis in "xyz"]
    for stage, peers in enumerate(rings + [[sibling(pos)]]):
        e_send[stage] = total
        incoming = [
            start(e_send.at[stage], e_recv.at[stage, slot], there)
            for slot, there in enumerate(peers)
        ]
        for slot, copy in enumerate(incoming):
            copy.wait_recv()
            total = total + e_recv[stage, slot]
    energy_ref[...] = jnp.broadcast_to(jnp.sum(total, keepdims=True), energy_ref.shape)
    for distance, copy in enumerate(block_in, 1):
        copy.wait_recv()
        other = (batch + count - distance) % count
        block = a_ref.at[own_rows, columns(other)]
        aside.append(start(block, block, sibling(pos)))
    own_block.wait()
    for copy in x_in + aside:
        copy.wait_recv()
    for copy in made:
        copy.wait_send()


EXCHANGE_COPIES = 14 + 6 + 7 + 1 + 21 + 10 + 7


class Reduction:
    def __init__(self, pos, part, work, out, slots, copies):
        self.pos, self.part, self.work, self.out = pos, part, work, out
        self.slots, self.copies = slots, copies
        self.base = [CHIPS * sum(UNITS[:k]) for k in range(3)]

    def axis(self, k, stage):
        return ORDERS[k][stage]

    def size(self, k, stage):
        return (16, 4, 1)[stage] * UNITS[k]

    def origin(self, k, depth):
        start = self.base[k]
        for stage in range(depth):
            start = start + self.pos[self.axis(k, stage)] * self.size(k, stage)
        return start

    def peer(self, k, stage, d):
        return ring_peer(self.pos, self.axis(k, stage), d)

    def sum_copy(self, k, stage, d):
        size = self.size(k, stage)
        source = self.part if stage == 0 else self.work
        target = (self.pos[self.axis(k, stage)] + d) % RING
        return self.copies.copy(
            9 * k + 3 * stage + d - 1,
            source.at[span(self.origin(k, stage) + target * size, size, 8), :],
            self.slots[3 * k + stage].at[d - 1],
            self.peer(k, stage, d),
        )

    def gather_copy(self, k, stage, d):
        block = self.block(self.origin(k, stage + 1), self.size(k, stage))
        return self.copies.copy(27 + 9 * k + 3 * stage + d - 1, block, block, self.peer(k, stage, d))

    def block(self, start, size):
        return self.out.at[self.pos["core"], span(start, size, 8), :]

    def aside_copy(self, k, d):
        size = self.size(k, 0)
        sender = (self.pos[self.axis(k, 0)] + RING - d) % RING
        block = self.block(self.base[k] + sender * size, size)
        return self.copies.copy(54 + 4 * k + d, block, block, sibling(self.pos))

    def start(self, k):
        for d in (1, 2, 3):
            self.sum_copy(k, 0, d).start()

    def step(self, number):
        for k in range(3):
            if number < 3:
                stage = number
                for d in (1, 2, 3):
                    self.sum_copy(k, stage, d).wait_recv()
                here = span(self.origin(k, stage + 1), self.size(k, stage), 8)
                source = self.part if stage == 0 else self.work
                slot = self.slots[3 * k + stage]
                value = source[here, :] + slot[0] + slot[1] + slot[2]
                if stage < 2:
                    self.work[here, :] = value
                    for d in (1, 2, 3):
                        self.sum_copy(k, stage + 1, d).start()
                else:
                    self.out[self.pos["core"], here, :] = value
                    for d in (1, 2, 3):
                        self.gather_copy(k, 2, d).start()
            else:
                stage = 5 - number
                for d in (1, 2, 3):
                    self.gather_copy(k, stage, d).wait_recv()
                    if stage == 0:
                        self.aside_copy(k, d).start()
                if stage:
                    for d in (1, 2, 3):
                        self.gather_copy(k, stage - 1, d).start()
                if stage == 1:
                    self.aside_copy(k, 0).start()

    def finish(self):
        for k in range(3):
            for d in range(4):
                self.aside_copy(k, d).wait()
            for d in (1, 2, 3):
                for stage in range(3):
                    self.sum_copy(k, stage, d).wait_send()
                    self.gather_copy(k, stage, d).wait_send()


REDUCE_COPIES = 27 + 27 + 12


def apply_gram(a_ref, q_block, scale, part, reduction):
    chunks = part.shape[0] // 256
    q = jnp.concatenate([q_block(chunk) for chunk in range(chunks)], axis=1)
    inner = stack(fold(dot_low(stack(q), a_ref[...], NT)))
    ready = 0
    for block in range(chunks // 2):
        value = fold(dot_low(inner, a_ref[:, block * 256:(block + 1) * 256], NN))
        for half in range(2):
            chunk = 2 * block + half
            part[chunk * 256:(chunk + 1) * 256, :] = (
                value[:, half * 128:(half + 1) * 128] * scale
                + q_block(chunk) * (1.0 / CHIPS))
        while ready < 3 and CHIPS * sum(UNITS[:ready + 1]) <= (block + 1) * 512:
            reduction.start(ready)
            ready += 1


def factor_block(aug, work):
    row = lax.broadcasted_iota(jnp.int32, (8, NB), 0)
    height = 8 * GROUPS
    for panel in range(NB // height):
        low = height * panel
        left = [aug[low + 8 * g:low + 8 * g + 8, :NB] for g in range(GROUPS)]
        right = [aug[low + 8 * g:low + 8 * g + 8, NB:] for g in range(GROUPS)]
        for s in range(GROUPS):
            rest = range(s, GROUPS)
            lane = low + 8 * s
            cols = {
                (g, k): jnp.broadcast_to(left[g][:, lane + k:lane + k + 1], (8, NB))
                for g in rest for k in range(8)
            }
            pivots = jnp.zeros((8, NB), F32)
            for k in range(8):
                pivot = jnp.broadcast_to(cols[s, k][k:k + 1, :], (8, NB))
                inverse = 1.0 / pivot
                pivots = jnp.where(row == k, pivot, pivots)
                mult = {g: cols[g, k] * inverse for g in rest}
                mult[s] = jnp.where(row > k, mult[s], 0.0)
                for j in range(k + 1, 8):
                    value = jnp.broadcast_to(cols[s, j][k:k + 1, :], (8, NB))
                    for g in rest:
                        cols[g, j] = cols[g, j] - mult[g] * value
                left_row = jnp.broadcast_to(left[s][k:k + 1, :], (8, NB))
                right_row = jnp.broadcast_to(right[s][k:k + 1, :], (8, NB))
                for g in rest:
                    left[g] = left[g] - mult[g] * left_row
                    right[g] = right[g] - mult[g] * right_row
            scale = lax.rsqrt(pivots)
            work[lane:lane + 8, :NB] = left[s] * scale
            work[lane:lane + 8, NB:] = right[s] * scale
        if low + height < NB:
            rows = work[low:low + height, :]
            aug[low + height:, :] = (
                aug[low + height:, :] - dot_f32(rows[:, :NB], rows, TN)[low + height:, :])


def inverse_factor(z_ref, rest, lower, aug, work, hooks=()):
    n = rest.shape[0]
    blocks = n // NB
    z_ref[...] = jnp.zeros_like(z_ref)
    row = lax.broadcasted_iota(jnp.int32, (NB, NB), 0)
    col = lax.broadcasted_iota(jnp.int32, (NB, NB), 1)

    @pl.loop(0, blocks)
    def _(j):
        here = span(j * NB, NB, NB)
        aug[:, :NB] = rest[here, here]
        aug[:, NB:] = jnp.where(row == col, 1.0, 0.0)
        factor_block(aug, work)
        for block in range(blocks):
            @pl.when(j == block)
            def _():
                low, high = block * NB, (block + 1) * NB
                inverse = jnp.where(row >= col, work[:, NB:], 0.0)
                z_ref[low:high, low:high] = inverse
                if high < n:
                    column = dot_f32(rest[high:, low:high], inverse, NT)
                    lower[high:, low:high] = column
                    rest[high:, high:] = rest[high:, high:] - dot_f32(column, column, NT)
                if low:
                    z_ref[low:high, :low] = -dot_f32(
                        inverse, dot_f32(lower[low:high, :low], z_ref[:low, :low], NN), NN)
                if block < len(hooks):
                    for hook in hooks[block]:
                        hook()


def whole_kernel(bases_ref, start_ref, modes_ref, *scratch):
    (turned, a_ref, q_ref, energy, e_send, e_recv, part, work, first, second, lifted,
     z_ref, rest, lower, aug, factor_work) = scratch[:16]
    slots = scratch[16:34]
    sems = scratch[34:40]
    own_sem = scratch[40]
    pos = position()
    core = pos["core"]
    turned[...] = start_ref[...].T
    peers = batch_partners(pos, lax.axis_index("batch"), lax.axis_size("batch"))
    peers += [ring_peer(pos, "x", d) for d in (1, 2, 3)]
    peers += [ring_peer(pos, "z", d) for d in (1, 3)] + [sibling(pos)]
    greet(peers)
    exchange(
        pos, bases_ref, turned, a_ref, q_ref, energy, e_send, e_recv,
        Copies(sems[0], sems[1]), own_sem,
    )
    n, all_columns = lifted.shape
    chunks = all_columns // NB
    scale = all_columns / energy[0:1, :]

    reduction = Reduction(pos, part.at[0], work.at[0], first, slots[:9], Copies(*sems[2:4]))
    apply_gram(a_ref, lambda chunk: q_ref[chunk], scale, part.at[0], reduction)
    for number in range(6):
        reduction.step(number)
    reduction.finish()

    reduction = Reduction(pos, part.at[1], work.at[1], second, slots[9:], Copies(*sems[4:]))
    apply_gram(
        a_ref, lambda chunk: first[core, chunk * 256:(chunk + 1) * 256, :], scale,
        part.at[1], reduction,
    )

    def side(ref, half):
        return jnp.concatenate(
            [ref[half, chunk * 256:(chunk + 1) * 256, :] for chunk in range(chunks)], axis=1)

    low = jnp.concatenate([side(first, half).astype(BF16) for half in range(2)], axis=0)
    rest[...] = dot_low(low, low, NT)
    step = [functools.partial(reduction.step, number) for number in range(6)]
    inverse_factor(
        z_ref, rest, lower, aug, factor_work, [[], step[:1], step[1:2], step[2:4]])
    step[4]()
    step[5]()
    reduction.finish()

    def times_factor(value_high, value_low, rows):
        z_stack = stack(z_ref[rows, :rows.stop])
        z_high = z_stack[:rows.stop - rows.start]
        return (fold(dot_low(z_stack, value_high[:rows.stop], NN))
                + dot_low(z_high, value_low[:rows.stop], NN))

    halves = [slice(0, n // 2), slice(n // 2, n)]
    blocks = 4
    width = all_columns // blocks
    rest[...] = jnp.zeros_like(rest)
    for block in range(blocks):
        value = jnp.concatenate(
            [jnp.concatenate(
                [second[half, chunk * 256:(chunk + 1) * 256, :]
                 for chunk in range(block * chunks // blocks, (block + 1) * chunks // blocks)],
                axis=1) for half in range(2)], axis=0)
        value_high, value_low = split(value)
        value = jnp.concatenate(
            [times_factor(value_high, value_low, rows) for rows in halves], axis=0)
        lifted[:, block * width:(block + 1) * width] = value
    both = stack(lifted[...])
    both = dot_low(both, both[:n], NT)
    rest[...] = both[:n] + both[n:] + both[n:].T
    inverse_factor(z_ref, rest, lower, aug, factor_work)

    height = modes_ref.shape[0]
    own_rows = span(core * height, height, 16)
    total = jnp.zeros(modes_ref.shape, F32)
    for block in range(blocks):
        here = slice(block * width, (block + 1) * width)
        value_high, value_low = split(lifted[:, here])
        q_low = jnp.concatenate(
            [times_factor(value_high, value_low, rows) for rows in halves], axis=0
        ).astype(BF16)
        total = total + dot_low(a_ref[own_rows, here], q_low, NT)
    modes_ref[...] = total.astype(BF16)


def on_device(bases, start):
    count = lax.axis_size("batch")
    width, n = start.shape
    all_columns = width * count
    height = bases.shape[0] // count
    flat = all_columns * n // 2 // 128
    sems = lambda number: [pltpu.SemaphoreType.DMA((number,))] * 2
    slots = [pltpu.VMEM((3, size * u, 128), F32) for u in UNITS for size in (16, 4, 1)]
    return pl.pallas_call(
        whole_kernel,
        out_shape=jax.ShapeDtypeStruct((height, n), BF16),
        in_specs=[VMEM_SPEC] * 2,
        out_specs=VMEM_SPEC,
        scratch_shapes=[
            pltpu.VMEM((n, width), F32),
            pltpu.VMEM((2 * height, all_columns), BF16),
            pltpu.VMEM((flat // 256, 256, 128), F32),
            pltpu.VMEM((8, 128), F32),
            pltpu.VMEM((4, 8, 128), F32),
            pltpu.VMEM((4, 3, 8, 128), F32),
            pltpu.VMEM((2, flat, 128), F32),
            pltpu.VMEM((2, flat, 128), F32),
            pltpu.VMEM((2, flat, 128), F32),
            pltpu.VMEM((2, flat, 128), F32),
            pltpu.VMEM((n, all_columns), F32),
            pltpu.VMEM((n, n), F32),
            pltpu.VMEM((n, n), F32),
            pltpu.VMEM((n, n), F32),
            pltpu.VMEM((NB, 2 * NB), F32),
            pltpu.VMEM((NB, 2 * NB), F32),
            *slots, *slots,
            *sems(EXCHANGE_COPIES), *sems(REDUCE_COPIES), *sems(REDUCE_COPIES),
            pltpu.SemaphoreType.DMA((3,)),
        ],
        compiler_params=pltpu.CompilerParams(
            collective_id=0, has_side_effects=True, vmem_limit_bytes=66_000_000
        ),
    )(bases, start)


def solution(mesh):
    in_specs = (P("rows", "batch"), P("batch", None))
    out_specs = P(("rows", "batch"), None)
    return jax.shard_map(
        on_device, mesh=mesh, in_specs=in_specs, out_specs=out_specs, check_vma=False
    )
```

time: 1050 us -> 175 us (0.17)
  waiting for transfers between devices: 616 us -> 0 us
  other arithmetic: 246 us -> 0 us
  Pallas kernels: 0 us -> 173 us
  blocking collectives: 79.2 us -> 0 us
  matrix products: 50.5 us -> 0 us
  local copies, waits for them, and re-layouts: 32.1 us -> 1.77 us
  between operations: 20.1 us -> 0.01 us
    psum x3 -> x0, waiting for transfers between devices: 272 us -> none  [the longest x2 164 us: on_device(): correlation = lax.psum(local_correlation, 'batch')]
    all_gather x3 -> x0, waiting for transfers between devices: 240 us -> none  [the longest x1 166 us: on_device(): lax.all_gather(bases, 'batch', axis=1, tiled=True)]
    another operation x34 -> x0, other arithmetic: 239 us -> none  [the longest x29 158 us: on_device(): factor = jnp.linalg.cholesky(correlation)]
    pallas_call x0 -> x1, Pallas kernels: none -> 173 us  [on_device(): pl.pallas_call(whole_kernel, out_shape=jax.ShapeDtypeStruct((height, n),...]
    reduce_scatter x1 -> x0, waiting for transfers between devices: 102 us -> none  [on_device(): lax.psum_scatter(jnp.dot(bases, q_low, preferred_element_type=jnp.float32...]
    psum x1 -> x0, blocking collectives: 79.2 us -> none  [on_device(): lax.psum(jnp.sum(jnp.square(bases.astype(jnp.float32))), ('rows', 'batch'))]
    dot_general x6 -> x0, matrix products: 28.2 us -> none  [the longest x2 12.5 us: on_device(): jnp.dot(gram_rows, q_full, precision=lax.Precision.HIGHEST) / diag_mean]
    another operation x38 -> x0, local copies, waits for them, and re-layouts: 23.8 us -> none  [the longest x30 23.6 us: on_device(): q_own = jax.scipy.linalg.solve_triangular(factor, lifted.T, lower=True).T]
  transfers between devices with their start and end apart: 7 -> 0, of which waited for: 6 -> 0; matrix products, arithmetic and copies ran while one was open for 1% -> 0% of each run, Pallas kernels for 0% -> 0%
where the time goes in v2:
time: 175 us
  Pallas kernels  173 us (99%)
  local copies, waits for them, and re-layouts  1.77 us (1%)
    pallas_call x1, Pallas kernels, on_device(): pl.pallas_call(whole_kernel, out_shape=jax.ShapeDtypeStruct((height, n),...  173 us

profile of v2, /device:TPU:1, one launch (start us, length us, event | category | flops | bytes accessed | tf_op | source)
XLA Modules:
  0.0 174.9 jit_solution(16701847527402425297)
XLA Ops:
  0.0 173.1 %shard_map.28 = bf16[384,512]{1,0:T(8,128)(2,1)} custom-call(bf16[3072,256]{1,0:T(8,128)(2,1)} %bases_ref.1, f32[256,512]{1,0:T(8,128)} %start_ref.1), custom_call_target="tpu_custom_call" | custom-call | tf_op jit(solution)/shard_map/pallas_call | solution.py:489
  173.1 1.8 %copy.4 = bf16[384,512]{1,0:T(8,128)(2,1)} copy(bf16[384,512]{1,0:T(8,128)(2,1)} %shard_map.28) | data formatting | bytes 786432

commit v3 on v2

--- a/solution.py
+++ b/solution.py
@@ -11,8 +11,9 @@
 GROUPS = 8
 RING = 4
 CHIPS = 64
-ORDERS = (("x", "y", "z"), ("y", "z", "x"), ("z", "x", "y"))
-UNITS = (24, 24, 16)
+ORDERS = (("x", "y", "z"), ("y", "z", "x"), ("z", "x", "y")) * 2
+UNITS = (16, 8, 8, 8, 16, 8)
+COLOURS = len(UNITS)
 HIGHEST = lax.Precision.HIGHEST
 VMEM_SPEC = pl.BlockSpec(memory_space=pltpu.VMEM)
 F32, BF16 = jnp.float32, jnp.bfloat16
@@ -181,6 +182,23 @@
     )
     total = total[:, :128] + total[:, 128:]
 
+    rings = [[ring_peer(pos, axis, d) for d in (1, 2, 3)] for axis in "xyz"]
+    rings.append([sibling(pos)])
+
+    def send_energy(stage, total):
+        e_send[stage] = total
+        return [
+            start(e_send.at[stage], e_recv.at[stage, slot], there)
+            for slot, there in enumerate(rings[stage])
+        ]
+
+    def add_energy(stage, incoming, total):
+        for slot, copy in enumerate(incoming):
+            copy.wait_recv()
+            total = total + e_recv[stage, slot]
+        return total
+
+    incoming = send_energy(0, total)
     for distance, pair in enumerate(start_in, 1):
         for copy in pair:
             copy.wait_recv()
@@ -189,23 +207,19 @@
         x_in += [start(block, block, there) for there in x_peers]
     for copy in own_start:
         copy.wait()
-    rings = [[ring_peer(pos, axis, d) for d in (1, 2, 3)] for axis in "xyz"]
-    for stage, peers in enumerate(rings + [[sibling(pos)]]):
-        e_send[stage] = total
-        incoming = [
-            start(e_send.at[stage], e_recv.at[stage, slot], there)
-            for slot, there in enumerate(peers)
-        ]
-        for slot, copy in enumerate(incoming):
-            copy.wait_recv()
-            total = total + e_recv[stage, slot]
-    energy_ref[...] = jnp.broadcast_to(jnp.sum(total, keepdims=True), energy_ref.shape)
+    own_block.wait()
+    stage = 0
     for distance, copy in enumerate(block_in, 1):
+        if distance % 2:
+            total = add_energy(stage, incoming, total)
+            stage += 1
+            if stage < 4:
+                incoming = send_energy(stage, total)
         copy.wait_recv()
         other = (batch + count - distance) % count
         block = a_ref.at[own_rows, columns(other)]
         aside.append(start(block, block, sibling(pos)))
-    own_block.wait()
+    energy_ref[...] = jnp.broadcast_to(jnp.sum(total, keepdims=True), energy_ref.shape)
     for copy in x_in + aside:
         copy.wait_recv()
     for copy in made:
@@ -219,7 +233,7 @@
     def __init__(self, pos, part, work, out, slots, copies):
         self.pos, self.part, self.work, self.out = pos, part, work, out
         self.slots, self.copies = slots, copies
-        self.base = [CHIPS * sum(UNITS[:k]) for k in range(3)]
+        self.base = [CHIPS * sum(UNITS[:k]) for k in range(COLOURS)]
 
     def axis(self, k, stage):
         return ORDERS[k][stage]
@@ -249,7 +263,7 @@
 
     def gather_copy(self, k, stage, d):
         block = self.block(self.origin(k, stage + 1), self.size(k, stage))
-        return self.copies.copy(27 + 9 * k + 3 * stage + d - 1, block, block, self.peer(k, stage, d))
+        return self.copies.copy(9 * COLOURS + 9 * k + 3 * stage + d - 1, block, block, self.peer(k, stage, d))
 
     def block(self, start, size):
         return self.out.at[self.pos["core"], span(start, size, 8), :]
@@ -258,14 +272,14 @@
         size = self.size(k, 0)
         sender = (self.pos[self.axis(k, 0)] + RING - d) % RING
         block = self.block(self.base[k] + sender * size, size)
-        return self.copies.copy(54 + 4 * k + d, block, block, sibling(self.pos))
+        return self.copies.copy(18 * COLOURS + 4 * k + d, block, block, sibling(self.pos))
 
     def start(self, k):
         for d in (1, 2, 3):
             self.sum_copy(k, 0, d).start()
 
-    def step(self, number):
-        for k in range(3):
+    def step(self, number, colours=range(COLOURS)):
+        for k in colours:
             if number < 3:
                 stage = number
                 for d in (1, 2, 3):
@@ -294,17 +308,22 @@
                 if stage == 1:
                     self.aside_copy(k, 0).start()
 
+    def join(self):
+        for k in range(COLOURS):
+            for d in range(4):
+                self.aside_copy(k, d).wait_recv()
+
     def finish(self):
-        for k in range(3):
+        for k in range(COLOURS):
             for d in range(4):
-                self.aside_copy(k, d).wait()
+                self.aside_copy(k, d).wait_send()
             for d in (1, 2, 3):
                 for stage in range(3):
                     self.sum_copy(k, stage, d).wait_send()
                     self.gather_copy(k, stage, d).wait_send()
 
 
-REDUCE_COPIES = 27 + 27 + 12
+REDUCE_COPIES = (9 + 9 + 4) * COLOURS
 
 
 def apply_gram(a_ref, q_block, scale, part, reduction):
@@ -319,12 +338,12 @@
             part[chunk * 256:(chunk + 1) * 256, :] = (
                 value[:, half * 128:(half + 1) * 128] * scale
                 + q_block(chunk) * (1.0 / CHIPS))
-        while ready < 3 and CHIPS * sum(UNITS[:ready + 1]) <= (block + 1) * 512:
+        while ready < COLOURS and CHIPS * sum(UNITS[:ready + 1]) <= (block + 1) * 512:
             reduction.start(ready)
             ready += 1
 
 
-def factor_block(aug, work):
+def factor_block(aug, work, between=lambda: None):
     row = lax.broadcasted_iota(jnp.int32, (8, NB), 0)
     height = 8 * GROUPS
     for panel in range(NB // height):
@@ -361,9 +380,10 @@
             rows = work[low:low + height, :]
             aug[low + height:, :] = (
                 aug[low + height:, :] - dot_f32(rows[:, :NB], rows, TN)[low + height:, :])
-
-
-def inverse_factor(z_ref, rest, lower, aug, work, hooks=()):
+            between()
+
+
+def inverse_factor(z_ref, rest, lower, aug, work, hooks={}):
     n = rest.shape[0]
     blocks = n // NB
     z_ref[...] = jnp.zeros_like(z_ref)
@@ -375,7 +395,13 @@
         here = span(j * NB, NB, NB)
         aug[:, :NB] = rest[here, here]
         aug[:, NB:] = jnp.where(row == col, 1.0, 0.0)
-        factor_block(aug, work)
+
+        def between():
+            for block in range(blocks):
+                if (block, 0) in hooks:
+                    pl.when(j == block)(hooks[block, 0])
+
+        factor_block(aug, work, between)
         for block in range(blocks):
             @pl.when(j == block)
             def _():
@@ -389,17 +415,13 @@
                 if low:
                     z_ref[low:high, :low] = -dot_f32(
                         inverse, dot_f32(lower[low:high, :low], z_ref[:low, :low], NN), NN)
-                if block < len(hooks):
-                    for hook in hooks[block]:
-                        hook()
+                hooks.get((block, 1), lambda: None)()
 
 
 def whole_kernel(bases_ref, start_ref, modes_ref, *scratch):
     (turned, a_ref, q_ref, energy, e_send, e_recv, part, work, first, second, lifted,
      z_ref, rest, lower, aug, factor_work) = scratch[:16]
-    slots = scratch[16:34]
-    sems = scratch[34:40]
-    own_sem = scratch[40]
+    slots, sems, own_sem = scratch[16:-7], scratch[-7:-1], scratch[-1]
     pos = position()
     core = pos["core"]
     turned[...] = start_ref[...].T
@@ -415,13 +437,13 @@
     chunks = all_columns // NB
     scale = all_columns / energy[0:1, :]
 
-    reduction = Reduction(pos, part.at[0], work.at[0], first, slots[:9], Copies(*sems[2:4]))
+    reduction = Reduction(pos, part.at[0], work.at[0], first, slots[:3 * COLOURS], Copies(*sems[2:4]))
+    early = reduction
     apply_gram(a_ref, lambda chunk: q_ref[chunk], scale, part.at[0], reduction)
     for number in range(6):
         reduction.step(number)
-    reduction.finish()
-
-    reduction = Reduction(pos, part.at[1], work.at[1], second, slots[9:], Copies(*sems[4:]))
+
+    reduction = Reduction(pos, part.at[1], work.at[1], second, slots[3 * COLOURS:], Copies(*sems[4:]))
     apply_gram(
         a_ref, lambda chunk: first[core, chunk * 256:(chunk + 1) * 256, :], scale,
         part.at[1], reduction,
@@ -431,14 +453,18 @@
         return jnp.concatenate(
             [ref[half, chunk * 256:(chunk + 1) * 256, :] for chunk in range(chunks)], axis=1)
 
+    early.join()
     low = jnp.concatenate([side(first, half).astype(BF16) for half in range(2)], axis=0)
     rest[...] = dot_low(low, low, NT)
-    step = [functools.partial(reduction.step, number) for number in range(6)]
+    sets = [range(3), range(3, 6)]
     inverse_factor(
-        z_ref, rest, lower, aug, factor_work, [[], step[:1], step[1:2], step[2:4]])
-    step[4]()
-    step[5]()
-    reduction.finish()
+        z_ref, rest, lower, aug, factor_work,
+        {(stage + 1, part): functools.partial(reduction.step, stage, sets[part])
+         for stage in range(3) for part in range(2)},
+    )
+    for stage in (3, 4, 5):
+        reduction.step(stage)
+    reduction.join()
 
     def times_factor(value_high, value_low, rows):
         z_stack = stack(z_ref[rows, :rows.stop])
@@ -476,6 +502,8 @@
         ).astype(BF16)
         total = total + dot_low(a_ref[own_rows, here], q_low, NT)
     modes_ref[...] = total.astype(BF16)
+    early.finish()
+    reduction.finish()
 
 
 def on_device(bases, start):

time: 175 us -> 163 us (0.931)
  Pallas kernels: 173 us -> 161 us
    pallas_call x1, Pallas kernels: 173 us -> 161 us  [on_device(): pl.pallas_call(whole_kernel, out_shape=jax.ShapeDtypeStruct((height, n),...]
where the time goes in v3:
time: 163 us
  Pallas kernels  161 us (99%)
  local copies, waits for them, and re-layouts  1.77 us (1%)
    pallas_call x1, Pallas kernels, on_device(): pl.pallas_call(whole_kernel, out_shape=jax.ShapeDtypeStruct((height, n),...  161 us

profile of v3, /device:TPU:1, one launch (start us, length us, event | category | flops | bytes accessed | tf_op | source)
XLA Modules:
  0.0 162.9 jit_solution(11696200182372342418)
XLA Ops:
  0.0 161.1 %shard_map.28 = bf16[384,512]{1,0:T(8,128)(2,1)} custom-call(bf16[3072,256]{1,0:T(8,128)(2,1)} %bases_ref.1, f32[256,512]{1,0:T(8,128)} %start_ref.1), custom_call_target="tpu_custom_call" | custom-call | tf_op jit(solution)/shard_map/pallas_call | solution.py:517
  161.1 1.8 %copy.4 = bf16[384,512]{1,0:T(8,128)(2,1)} copy(bf16[384,512]{1,0:T(8,128)(2,1)} %shard_map.28) | data formatting | bytes 786432

commit v4 on v3

--- a/solution.py
+++ b/solution.py
@@ -77,12 +77,13 @@
     return there
 
 
-def greet(peers):
+def greet(peers, work):
     barrier = pltpu.get_barrier_semaphore()
     for peer in peers:
         pl.semaphore_signal(
             barrier, inc=1, device_id=device_at(peer), device_id_type=pl.DeviceIdType.MESH
         )
+    work()
     pl.semaphore_wait(barrier, len(peers))
 
 
@@ -109,9 +110,7 @@
     return partners
 
 
-def exchange(
-    pos, bases_ref, turned, a_ref, q_ref, energy_ref, e_send, e_recv, copies, own_sem
-):
+def exchange(pos, bases_ref, turned, a_ref, q_ref, energy, copies, own_sem):
     core, x = pos["core"], pos["x"]
     batch = lax.axis_index("batch")
     count = lax.axis_size("batch")
@@ -182,23 +181,7 @@
     )
     total = total[:, :128] + total[:, 128:]
 
-    rings = [[ring_peer(pos, axis, d) for d in (1, 2, 3)] for axis in "xyz"]
-    rings.append([sibling(pos)])
-
-    def send_energy(stage, total):
-        e_send[stage] = total
-        return [
-            start(e_send.at[stage], e_recv.at[stage, slot], there)
-            for slot, there in enumerate(rings[stage])
-        ]
-
-    def add_energy(stage, incoming, total):
-        for slot, copy in enumerate(incoming):
-            copy.wait_recv()
-            total = total + e_recv[stage, slot]
-        return total
-
-    incoming = send_energy(0, total)
+    energy.begin(total)
     for distance, pair in enumerate(start_in, 1):
         for copy in pair:
             copy.wait_recv()
@@ -208,30 +191,58 @@
     for copy in own_start:
         copy.wait()
     own_block.wait()
-    stage = 0
     for distance, copy in enumerate(block_in, 1):
-        if distance % 2:
-            total = add_energy(stage, incoming, total)
-            stage += 1
-            if stage < 4:
-                incoming = send_energy(stage, total)
         copy.wait_recv()
         other = (batch + count - distance) % count
         block = a_ref.at[own_rows, columns(other)]
         aside.append(start(block, block, sibling(pos)))
-    energy_ref[...] = jnp.broadcast_to(jnp.sum(total, keepdims=True), energy_ref.shape)
     for copy in x_in + aside:
         copy.wait_recv()
     for copy in made:
         copy.wait_send()
 
 
-EXCHANGE_COPIES = 14 + 6 + 7 + 1 + 21 + 10 + 7
+EXCHANGE_COPIES = 14 + 6 + 7 + 1 + 21 + 7
+
+
+class Energy:
+    def __init__(self, pos, sums, slots, copies):
+        self.sums, self.slots, self.copies = sums, slots, copies
+        self.rings = [[ring_peer(pos, axis, d) for d in (1, 2, 3)] for axis in "xyz"]
+        self.rings.append([sibling(pos)])
+
+    def copy(self, stage, slot):
+        return self.copies.copy(
+            3 * stage + slot, self.sums.at[stage], self.slots.at[stage, slot],
+            self.rings[stage][slot],
+        )
+
+    def begin(self, total):
+        self.sums[0] = total
+        for slot in range(3):
+            self.copy(0, slot).start()
+
+    def step(self, stage):
+        total = self.sums[stage]
+        for slot in range(len(self.rings[stage])):
+            self.copy(stage, slot).wait()
+            total = total + self.slots[stage, slot]
+        self.sums[stage + 1] = total
+        if stage < 3:
+            for slot in range(len(self.rings[stage + 1])):
+                self.copy(stage + 1, slot).start()
+
+    def value(self):
+        return jnp.sum(self.sums[4], keepdims=True)
+
+
+ENERGY_COPIES = 10
 
 
 class Reduction:
-    def __init__(self, pos, part, work, out, slots, copies):
+    def __init__(self, pos, part, part_low, work, out, slots, copies, forward):
         self.pos, self.part, self.work, self.out = pos, part, work, out
+        self.part_low, self.forward = part_low, forward
         self.slots, self.copies = slots, copies
         self.base = [CHIPS * sum(UNITS[:k]) for k in range(COLOURS)]
 
@@ -252,11 +263,11 @@
 
     def sum_copy(self, k, stage, d):
         size = self.size(k, stage)
-        source = self.part if stage == 0 else self.work
+        source = self.part_low if stage == 0 else self.work
         target = (self.pos[self.axis(k, stage)] + d) % RING
         return self.copies.copy(
             9 * k + 3 * stage + d - 1,
-            source.at[span(self.origin(k, stage) + target * size, size, 8), :],
+            source.at[span(self.origin(k, stage) + target * size, size, 8 if stage else 16), :],
             self.slots[3 * k + stage].at[d - 1],
             self.peer(k, stage, d),
         )
@@ -287,7 +298,9 @@
                 here = span(self.origin(k, stage + 1), self.size(k, stage), 8)
                 source = self.part if stage == 0 else self.work
                 slot = self.slots[3 * k + stage]
-                value = source[here, :] + slot[0] + slot[1] + slot[2]
+                value = source[here, :]
+                for d in range(3):
+                    value = value + slot[d].astype(F32)
                 if stage < 2:
                     self.work[here, :] = value
                     for d in (1, 2, 3):
@@ -300,12 +313,12 @@
                 stage = 5 - number
                 for d in (1, 2, 3):
                     self.gather_copy(k, stage, d).wait_recv()
-                    if stage == 0:
+                    if stage == 0 and self.forward:
                         self.aside_copy(k, d).start()
                 if stage:
                     for d in (1, 2, 3):
                         self.gather_copy(k, stage - 1, d).start()
-                if stage == 1:
+                if stage == 1 and self.forward:
                     self.aside_copy(k, 0).start()
 
     def join(self):
@@ -315,8 +328,9 @@
 
     def finish(self):
         for k in range(COLOURS):
-            for d in range(4):
-                self.aside_copy(k, d).wait_send()
+            if self.forward:
+                for d in range(4):
+                    self.aside_copy(k, d).wait_send()
             for d in (1, 2, 3):
                 for stage in range(3):
                     self.sum_copy(k, stage, d).wait_send()
@@ -326,8 +340,8 @@
 REDUCE_COPIES = (9 + 9 + 4) * COLOURS
 
 
-def apply_gram(a_ref, q_block, scale, part, reduction):
-    chunks = part.shape[0] // 256
+def apply_gram(a_ref, q_block, combine, reduction):
+    chunks = a_ref.shape[1] // 128
     q = jnp.concatenate([q_block(chunk) for chunk in range(chunks)], axis=1)
     inner = stack(fold(dot_low(stack(q), a_ref[...], NT)))
     ready = 0
@@ -335,9 +349,10 @@
         value = fold(dot_low(inner, a_ref[:, block * 256:(block + 1) * 256], NN))
         for half in range(2):
             chunk = 2 * block + half
-            part[chunk * 256:(chunk + 1) * 256, :] = (
-                value[:, half * 128:(half + 1) * 128] * scale
-                + q_block(chunk) * (1.0 / CHIPS))
+            share = combine(value[:, half * 128:(half + 1) * 128], chunk)
+            here = slice(chunk * 256, (chunk + 1) * 256)
+            reduction.part[here, :] = share
+            reduction.part_low[here, :] = share.astype(BF16)
         while ready < COLOURS and CHIPS * sum(UNITS[:ready + 1]) <= (block + 1) * 512:
             reduction.start(ready)
             ready += 1
@@ -419,41 +434,65 @@
 
 
 def whole_kernel(bases_ref, start_ref, modes_ref, *scratch):
-    (turned, a_ref, q_ref, energy, e_send, e_recv, part, work, first, second, lifted,
-     z_ref, rest, lower, aug, factor_work) = scratch[:16]
-    slots, sems, own_sem = scratch[16:-7], scratch[-7:-1], scratch[-1]
+    (slab, turned, a_ref, q_ref, e_sums, e_slots, part, part_low, work, first, second, lifted,
+     z_ref, rest, lower, aug, factor_work) = scratch[:17]
+    slots, sems, own_sem = scratch[17:-9], scratch[-9:-1], scratch[-1]
     pos = position()
     core = pos["core"]
-    turned[...] = start_ref[...].T
+    load = pltpu.make_async_copy(bases_ref, slab, own_sem.at[3])
+    load.start()
     peers = batch_partners(pos, lax.axis_index("batch"), lax.axis_size("batch"))
     peers += [ring_peer(pos, "x", d) for d in (1, 2, 3)]
     peers += [ring_peer(pos, "z", d) for d in (1, 3)] + [sibling(pos)]
-    greet(peers)
-    exchange(
-        pos, bases_ref, turned, a_ref, q_ref, energy, e_send, e_recv,
-        Copies(sems[0], sems[1]), own_sem,
-    )
+
+    def turn():
+        turned[...] = start_ref[...].T
+
+    greet(peers, turn)
+    load.wait()
+    energy = Energy(pos, e_sums, e_slots, Copies(*sems[6:]))
+    exchange(pos, slab, turned, a_ref, q_ref, energy, Copies(*sems[:2]), own_sem)
     n, all_columns = lifted.shape
     chunks = all_columns // NB
-    scale = all_columns / energy[0:1, :]
-
-    reduction = Reduction(pos, part.at[0], work.at[0], first, slots[:3 * COLOURS], Copies(*sems[2:4]))
+
+    reduction = Reduction(
+        pos, part.at[0], part_low.at[0], work.at[0], first, slots[:3 * COLOURS],
+        Copies(*sems[2:4]), False,
+    )
     early = reduction
-    apply_gram(a_ref, lambda chunk: q_ref[chunk], scale, part.at[0], reduction)
+    apply_gram(a_ref, lambda chunk: q_ref[chunk], lambda value, chunk: value, reduction)
     for number in range(6):
+        if number < 4:
+            energy.step(number)
         reduction.step(number)
-
-    reduction = Reduction(pos, part.at[1], work.at[1], second, slots[3 * COLOURS:], Copies(*sems[4:]))
+    early.finish()
+    scale = all_columns / energy.value()
+    for chunk in range(chunks):
+        here = slice(chunk * 256, (chunk + 1) * 256)
+        first[core, here, :] = first[core, here, :] * scale + q_ref[chunk]
+    over = Copies(*sems[2:4]).copy(
+        18 * COLOURS, first.at[core], first.at[core], sibling(pos)
+    )
+    over.start()
+
+    reduction = Reduction(
+        pos, part.at[1], part_low.at[1], work.at[1], second, slots[3 * COLOURS:],
+        Copies(*sems[4:6]), True,
+    )
+
+    def first_block(chunk):
+        return first[core, chunk * 256:(chunk + 1) * 256, :]
+
     apply_gram(
-        a_ref, lambda chunk: first[core, chunk * 256:(chunk + 1) * 256, :], scale,
-        part.at[1], reduction,
+        a_ref, first_block,
+        lambda value, chunk: value * scale + first_block(chunk) * (1.0 / CHIPS), reduction,
     )
 
     def side(ref, half):
         return jnp.concatenate(
             [ref[half, chunk * 256:(chunk + 1) * 256, :] for chunk in range(chunks)], axis=1)
 
-    early.join()
+    over.wait()
     low = jnp.concatenate([side(first, half).astype(BF16) for half in range(2)], axis=0)
     rest[...] = dot_low(low, low, NT)
     sets = [range(3), range(3, 6)]
@@ -502,7 +541,6 @@
         ).astype(BF16)
         total = total + dot_low(a_ref[own_rows, here], q_low, NT)
     modes_ref[...] = total.astype(BF16)
-    early.finish()
     reduction.finish()
 
 
@@ -513,20 +551,24 @@
     height = bases.shape[0] // count
     flat = all_columns * n // 2 // 128
     sems = lambda number: [pltpu.SemaphoreType.DMA((number,))] * 2
-    slots = [pltpu.VMEM((3, size * u, 128), F32) for u in UNITS for size in (16, 4, 1)]
+    slots = [
+        pltpu.VMEM((3, size * u, 128), BF16 if size == 16 else F32)
+        for u in UNITS for size in (16, 4, 1)
+    ]
     return pl.pallas_call(
         whole_kernel,
         out_shape=jax.ShapeDtypeStruct((height, n), BF16),
-        in_specs=[VMEM_SPEC] * 2,
+        in_specs=[pl.BlockSpec(memory_space=pl.ANY), VMEM_SPEC],
         out_specs=VMEM_SPEC,
         scratch_shapes=[
+            pltpu.VMEM(bases.shape, BF16),
             pltpu.VMEM((n, width), F32),
             pltpu.VMEM((2 * height, all_columns), BF16),
             pltpu.VMEM((flat // 256, 256, 128), F32),
-            pltpu.VMEM((8, 128), F32),
-            pltpu.VMEM((4, 8, 128), F32),
+            pltpu.VMEM((5, 8, 128), F32),
             pltpu.VMEM((4, 3, 8, 128), F32),
             pltpu.VMEM((2, flat, 128), F32),
+            pltpu.VMEM((2, flat, 128), BF16),
             pltpu.VMEM((2, flat, 128), F32),
             pltpu.VMEM((2, flat, 128), F32),
             pltpu.VMEM((2, flat, 128), F32),
@@ -538,7 +580,8 @@
             pltpu.VMEM((NB, 2 * NB), F32),
             *slots, *slots,
             *sems(EXCHANGE_COPIES), *sems(REDUCE_COPIES), *sems(REDUCE_COPIES),
-            pltpu.SemaphoreType.DMA((3,)),
+            *sems(ENERGY_COPIES),
+            pltpu.SemaphoreType.DMA((4,)),
         ],
         compiler_params=pltpu.CompilerParams(
             collective_id=0, has_side_effects=True, vmem_limit_bytes=66_000_000

time: 163 us -> 154 us (0.945)
  Pallas kernels: 161 us -> 152 us
    pallas_call x1, Pallas kernels: 161 us -> 152 us  [on_device(): pl.pallas_call(whole_kernel, out_shape=jax.ShapeDtypeStruct((height, n),...]
where the time goes in v4:
time: 154 us
  Pallas kernels  152 us (99%)
  local copies, waits for them, and re-layouts  1.77 us (1%)
    pallas_call x1, Pallas kernels, on_device(): pl.pallas_call(whole_kernel, out_shape=jax.ShapeDtypeStruct((height, n),...  152 us

profile of v4, /device:TPU:1, one launch (start us, length us, event | category | flops | bytes accessed | tf_op | source)
XLA Modules:
  0.0 153.7 jit_solution(15550198690893334861)
XLA Ops:
  0.0 151.9 %shard_map.28 = bf16[384,512]{1,0:T(8,128)(2,1)} custom-call(bf16[3072,256]{1,0:T(8,128)(2,1)} %bases_ref.1, f32[256,512]{1,0:T(8,128)} %start_ref.1), custom_call_target="tpu_custom_call" | custom-call | tf_op jit(solution)/shard_map/pallas_call | solution.py:558
  152.0 1.8 %copy.4 = bf16[384,512]{1,0:T(8,128)(2,1)} copy(bf16[384,512]{1,0:T(8,128)(2,1)} %shard_map.28) | data formatting | bytes 786432

commit v5 on v4

--- a/solution.py
+++ b/solution.py
@@ -69,6 +69,23 @@
     there = dict(pos)
     there[axis] = (pos[axis] + distance) % RING
     return there
+
+
+def shifted(pos, shifts):
+    there = dict(pos)
+    for axis, distance in shifts.items():
+        if distance:
+            there[axis] = (pos[axis] + distance) % RING
+    return there
+
+
+def neighbours(pos):
+    steps = range(RING)
+    shifts = [{"x": a, "y": b, "z": c} for a in steps for b in steps for c in steps]
+    return [
+        shifted(pos, shift) for shift in shifts
+        if 0 < sum(distance > 0 for distance in shift.values()) < 3
+    ] + [sibling(pos)]
 
 
 def sibling(pos):
@@ -239,6 +256,9 @@
 ENERGY_COPIES = 10
 
 
+PLANE = [(a, b) for a in range(RING) for b in range(RING) if a or b]
+
+
 class Reduction:
     def __init__(self, pos, part, part_low, work, out, slots, copies, forward):
         self.pos, self.part, self.work, self.out = pos, part, work, out
@@ -246,80 +266,92 @@
         self.slots, self.copies = slots, copies
         self.base = [CHIPS * sum(UNITS[:k]) for k in range(COLOURS)]
 
-    def axis(self, k, stage):
-        return ORDERS[k][stage]
-
-    def size(self, k, stage):
-        return (16, 4, 1)[stage] * UNITS[k]
-
-    def origin(self, k, depth):
-        start = self.base[k]
-        for stage in range(depth):
-            start = start + self.pos[self.axis(k, stage)] * self.size(k, stage)
-        return start
-
-    def peer(self, k, stage, d):
-        return ring_peer(self.pos, self.axis(k, stage), d)
-
-    def sum_copy(self, k, stage, d):
-        size = self.size(k, stage)
-        source = self.part_low if stage == 0 else self.work
-        target = (self.pos[self.axis(k, stage)] + d) % RING
-        return self.copies.copy(
-            9 * k + 3 * stage + d - 1,
-            source.at[span(self.origin(k, stage) + target * size, size, 8 if stage else 16), :],
-            self.slots[3 * k + stage].at[d - 1],
-            self.peer(k, stage, d),
-        )
-
-    def gather_copy(self, k, stage, d):
-        block = self.block(self.origin(k, stage + 1), self.size(k, stage))
-        return self.copies.copy(9 * COLOURS + 9 * k + 3 * stage + d - 1, block, block, self.peer(k, stage, d))
+    def first(self, k):
+        return self.pos[ORDERS[k][0]]
+
+    def origin(self, k):
+        return self.base[k] + self.first(k) * 16 * UNITS[k]
+
+    def place(self, k, a, b):
+        _, one, two = ORDERS[k]
+        index = (self.pos[one] + a) % RING * RING + (self.pos[two] + b) % RING
+        return self.origin(k) + index * UNITS[k]
+
+    def peer(self, k, a, b):
+        return shifted(self.pos, {ORDERS[k][1]: a, ORDERS[k][2]: b})
+
+    def ring_peer(self, k, d):
+        return ring_peer(self.pos, ORDERS[k][0], d)
 
     def block(self, start, size):
         return self.out.at[self.pos["core"], span(start, size, 8), :]
 
+    def ring_sum(self, k, d):
+        size = 16 * UNITS[k]
+        target = (self.first(k) + d) % RING
+        return self.copies.copy(
+            40 * k + d - 1, self.part_low.at[span(self.base[k] + target * size, size, 16), :],
+            self.slots[2 * k].at[d - 1], self.ring_peer(k, d),
+        )
+
+    def plane_sum(self, k, slot):
+        a, b = PLANE[slot]
+        return self.copies.copy(
+            40 * k + 3 + slot, self.work.at[span(self.place(k, a, b), UNITS[k], 8), :],
+            self.slots[2 * k + 1].at[slot], self.peer(k, a, b),
+        )
+
+    def plane_gather(self, k, slot):
+        block = self.block(self.place(k, 0, 0), UNITS[k])
+        return self.copies.copy(40 * k + 18 + slot, block, block, self.peer(k, *PLANE[slot]))
+
+    def ring_gather(self, k, d):
+        block = self.block(self.origin(k), 16 * UNITS[k])
+        return self.copies.copy(40 * k + 33 + d - 1, block, block, self.ring_peer(k, d))
+
     def aside_copy(self, k, d):
-        size = self.size(k, 0)
-        sender = (self.pos[self.axis(k, 0)] + RING - d) % RING
+        size = 16 * UNITS[k]
+        sender = (self.first(k) + RING - d) % RING
         block = self.block(self.base[k] + sender * size, size)
-        return self.copies.copy(18 * COLOURS + 4 * k + d, block, block, sibling(self.pos))
+        return self.copies.copy(40 * k + 36 + d, block, block, sibling(self.pos))
 
     def start(self, k):
         for d in (1, 2, 3):
-            self.sum_copy(k, 0, d).start()
+            self.ring_sum(k, d).start()
 
     def step(self, number, colours=range(COLOURS)):
         for k in colours:
-            if number < 3:
-                stage = number
+            if number == 0:
                 for d in (1, 2, 3):
-                    self.sum_copy(k, stage, d).wait_recv()
-                here = span(self.origin(k, stage + 1), self.size(k, stage), 8)
-                source = self.part if stage == 0 else self.work
-                slot = self.slots[3 * k + stage]
-                value = source[here, :]
+                    self.ring_sum(k, d).wait_recv()
+                here = span(self.origin(k), 16 * UNITS[k], 8)
+                value = self.part[here, :]
                 for d in range(3):
-                    value = value + slot[d].astype(F32)
-                if stage < 2:
-                    self.work[here, :] = value
-                    for d in (1, 2, 3):
-                        self.sum_copy(k, stage + 1, d).start()
-                else:
-                    self.out[self.pos["core"], here, :] = value
-                    for d in (1, 2, 3):
-                        self.gather_copy(k, 2, d).start()
+                    value = value + self.slots[2 * k][d].astype(F32)
+                self.work[here, :] = value
+                for slot in range(len(PLANE)):
+                    self.plane_sum(k, slot).start()
+            elif number == 1:
+                here = span(self.place(k, 0, 0), UNITS[k], 8)
+                value = self.work[here, :]
+                for slot in range(len(PLANE)):
+                    self.plane_sum(k, slot).wait_recv()
+                    value = value + self.slots[2 * k + 1][slot]
+                self.out[self.pos["core"], here, :] = value
+                for slot in range(len(PLANE)):
+                    self.plane_gather(k, slot).start()
+            elif number == 2:
+                for slot in range(len(PLANE)):
+                    self.plane_gather(k, slot).wait_recv()
+                for d in (1, 2, 3):
+                    self.ring_gather(k, d).start()
+                if self.forward:
+                    self.aside_copy(k, 0).start()
             else:
-                stage = 5 - number
                 for d in (1, 2, 3):
-                    self.gather_copy(k, stage, d).wait_recv()
-                    if stage == 0 and self.forward:
+                    self.ring_gather(k, d).wait_recv()
+                    if self.forward:
                         self.aside_copy(k, d).start()
-                if stage:
-                    for d in (1, 2, 3):
-                        self.gather_copy(k, stage - 1, d).start()
-                if stage == 1 and self.forward:
-                    self.aside_copy(k, 0).start()
 
     def join(self):
         for k in range(COLOURS):
@@ -332,12 +364,14 @@
                 for d in range(4):
                     self.aside_copy(k, d).wait_send()
             for d in (1, 2, 3):
-                for stage in range(3):
-                    self.sum_copy(k, stage, d).wait_send()
-                    self.gather_copy(k, stage, d).wait_send()
-
-
-REDUCE_COPIES = (9 + 9 + 4) * COLOURS
+                self.ring_sum(k, d).wait_send()
+                self.ring_gather(k, d).wait_send()
+            for slot in range(len(PLANE)):
+                self.plane_sum(k, slot).wait_send()
+                self.plane_gather(k, slot).wait_send()
+
+
+REDUCE_COPIES = 40 * COLOURS
 
 
 def apply_gram(a_ref, q_block, combine, reduction):
@@ -441,14 +475,10 @@
     core = pos["core"]
     load = pltpu.make_async_copy(bases_ref, slab, own_sem.at[3])
     load.start()
-    peers = batch_partners(pos, lax.axis_index("batch"), lax.axis_size("batch"))
-    peers += [ring_peer(pos, "x", d) for d in (1, 2, 3)]
-    peers += [ring_peer(pos, "z", d) for d in (1, 3)] + [sibling(pos)]
-
     def turn():
         turned[...] = start_ref[...].T
 
-    greet(peers, turn)
+    greet(neighbours(pos), turn)
     load.wait()
     energy = Energy(pos, e_sums, e_slots, Copies(*sems[6:]))
     exchange(pos, slab, turned, a_ref, q_ref, energy, Copies(*sems[:2]), own_sem)
@@ -456,14 +486,13 @@
     chunks = all_columns // NB
 
     reduction = Reduction(
-        pos, part.at[0], part_low.at[0], work.at[0], first, slots[:3 * COLOURS],
+        pos, part.at[0], part_low.at[0], work.at[0], first, slots[:2 * COLOURS],
         Copies(*sems[2:4]), False,
     )
     early = reduction
     apply_gram(a_ref, lambda chunk: q_ref[chunk], lambda value, chunk: value, reduction)
-    for number in range(6):
-        if number < 4:
-            energy.step(number)
+    for number in range(4):
+        energy.step(number)
         reduction.step(number)
     early.finish()
     scale = all_columns / energy.value()
@@ -471,12 +500,12 @@
         here = slice(chunk * 256, (chunk + 1) * 256)
         first[core, here, :] = first[core, here, :] * scale + q_ref[chunk]
     over = Copies(*sems[2:4]).copy(
-        18 * COLOURS, first.at[core], first.at[core], sibling(pos)
+        36, first.at[core], first.at[core], sibling(pos)
     )
     over.start()
 
     reduction = Reduction(
-        pos, part.at[1], part_low.at[1], work.at[1], second, slots[3 * COLOURS:],
+        pos, part.at[1], part_low.at[1], work.at[1], second, slots[2 * COLOURS:],
         Copies(*sems[4:6]), True,
     )
 
@@ -495,14 +524,13 @@
     over.wait()
     low = jnp.concatenate([side(first, half).astype(BF16) for half in range(2)], axis=0)
     rest[...] = dot_low(low, low, NT)
-    sets = [range(3), range(3, 6)]
+    places = [(0, 0), (0, 1), (1, 1), (2, 0), (2, 1), (3, 0)]
+    parts = [(number, range(3 * part, 3 * part + 3)) for number in range(3) for part in range(2)]
     inverse_factor(
         z_ref, rest, lower, aug, factor_work,
-        {(stage + 1, part): functools.partial(reduction.step, stage, sets[part])
-         for stage in range(3) for part in range(2)},
-    )
-    for stage in (3, 4, 5):
-        reduction.step(stage)
+        {place: functools.partial(reduction.step, *part) for place, part in zip(places, parts)},
+    )
+    reduction.step(3)
     reduction.join()
 
     def times_factor(value_high, value_low, rows):
@@ -551,10 +579,10 @@
     height = bases.shape[0] // count
     flat = all_columns * n // 2 // 128
     sems = lambda number: [pltpu.SemaphoreType.DMA((number,))] * 2
-    slots = [
-        pltpu.VMEM((3, size * u, 128), BF16 if size == 16 else F32)
-        for u in UNITS for size in (16, 4, 1)
-    ]
+    slots = []
+    for unit in UNITS:
+        slots.append(pltpu.VMEM((3, 16 * unit, 128), BF16))
+        slots.append(pltpu.VMEM((len(PLANE), unit, 128), F32))
     return pl.pallas_call(
         whole_kernel,
         out_shape=jax.ShapeDtypeStruct((height, n), BF16),

time: 154 us -> 147 us (0.955)
  Pallas kernels: 152 us -> 145 us
    pallas_call x1, Pallas kernels: 152 us -> 145 us  [on_device(): pl.pallas_call(whole_kernel, out_shape=jax.ShapeDtypeStruct((height, n),...]
where the time goes in v5:
time: 147 us
  Pallas kernels  145 us (99%)
  local copies, waits for them, and re-layouts  1.77 us (1%)
    pallas_call x1, Pallas kernels, on_device(): pl.pallas_call(whole_kernel, out_shape=jax.ShapeDtypeStruct((height, n),...  145 us

profile of v5, /device:TPU:1, one launch (start us, length us, event | category | flops | bytes accessed | tf_op | source)
XLA Modules:
  0.0 147.0 jit_solution(8604219823222187324)
XLA Ops:
  0.0 145.2 %shard_map.28 = bf16[384,512]{1,0:T(8,128)(2,1)} custom-call(bf16[3072,256]{1,0:T(8,128)(2,1)} %bases_ref.1, f32[256,512]{1,0:T(8,128)} %start_ref.1), custom_call_target="tpu_custom_call" | custom-call | tf_op jit(solution)/shard_map/pallas_call | solution.py:586
  145.2 1.8 %copy.4 = bf16[384,512]{1,0:T(8,128)(2,1)} copy(bf16[384,512]{1,0:T(8,128)(2,1)} %shard_map.28) | data formatting | bytes 786432

commit v6 on v5

--- a/solution.py
+++ b/solution.py
@@ -79,13 +79,8 @@
     return there
 
 
-def neighbours(pos):
-    steps = range(RING)
-    shifts = [{"x": a, "y": b, "z": c} for a in steps for b in steps for c in steps]
-    return [
-        shifted(pos, shift) for shift in shifts
-        if 0 < sum(distance > 0 for distance in shift.values()) < 3
-    ] + [sibling(pos)]
+def axis_peers(pos):
+    return [ring_peer(pos, axis, d) for axis in "xyz" for d in (1, 2, 3)]
 
 
 def sibling(pos):
@@ -470,7 +465,7 @@
 def whole_kernel(bases_ref, start_ref, modes_ref, *scratch):
     (slab, turned, a_ref, q_ref, e_sums, e_slots, part, part_low, work, first, second, lifted,
      z_ref, rest, lower, aug, factor_work) = scratch[:17]
-    slots, sems, own_sem = scratch[17:-9], scratch[-9:-1], scratch[-1]
+    slots, sems, own_sem, entered = scratch[17:-10], scratch[-10:-2], scratch[-2], scratch[-1]
     pos = position()
     core = pos["core"]
     load = pltpu.make_async_copy(bases_ref, slab, own_sem.at[3])
@@ -478,7 +473,14 @@
     def turn():
         turned[...] = start_ref[...].T
 
-    greet(neighbours(pos), turn)
+    peers = batch_partners(pos, lax.axis_index("batch"), lax.axis_size("batch"))
+    peers += [ring_peer(pos, "x", d) for d in (1, 2, 3)]
+    peers += [ring_peer(pos, "z", d) for d in (1, 3)] + [sibling(pos)]
+    greet(peers, turn)
+    for peer in axis_peers(pos):
+        pl.semaphore_signal(
+            entered, inc=1, device_id=device_at(peer), device_id_type=pl.DeviceIdType.MESH
+        )
     load.wait()
     energy = Energy(pos, e_sums, e_slots, Copies(*sems[6:]))
     exchange(pos, slab, turned, a_ref, q_ref, energy, Copies(*sems[:2]), own_sem)
@@ -491,6 +493,7 @@
     )
     early = reduction
     apply_gram(a_ref, lambda chunk: q_ref[chunk], lambda value, chunk: value, reduction)
+    pl.semaphore_wait(entered, 9)
     for number in range(4):
         energy.step(number)
         reduction.step(number)
@@ -524,13 +527,12 @@
     over.wait()
     low = jnp.concatenate([side(first, half).astype(BF16) for half in range(2)], axis=0)
     rest[...] = dot_low(low, low, NT)
-    places = [(0, 0), (0, 1), (1, 1), (2, 0), (2, 1), (3, 0)]
-    parts = [(number, range(3 * part, 3 * part + 3)) for number in range(3) for part in range(2)]
+    places = [(0, 0), (0, 1), (1, 0), (1, 1), (2, 0), (2, 1), (3, 0), (3, 1)]
+    parts = [(number, range(3 * part, 3 * part + 3)) for number in range(4) for part in range(2)]
     inverse_factor(
         z_ref, rest, lower, aug, factor_work,
         {place: functools.partial(reduction.step, *part) for place, part in zip(places, parts)},
     )
-    reduction.step(3)
     reduction.join()
 
     def times_factor(value_high, value_low, rows):
@@ -610,6 +612,7 @@
             *sems(EXCHANGE_COPIES), *sems(REDUCE_COPIES), *sems(REDUCE_COPIES),
             *sems(ENERGY_COPIES),
             pltpu.SemaphoreType.DMA((4,)),
+            pltpu.SemaphoreType.REGULAR,
         ],
         compiler_params=pltpu.CompilerParams(
             collective_id=0, has_side_effects=True, vmem_limit_bytes=66_000_000

time: 147 us -> 146 us (level)
  no operation moved by 1% of the time
where the time goes in v6:
time: 146 us
  Pallas kernels  144 us (99%)
  local copies, waits for them, and re-layouts  1.77 us (1%)
    pallas_call x1, Pallas kernels, on_device(): pl.pallas_call(whole_kernel, out_shape=jax.ShapeDtypeStruct((height, n),...  144 us

profile of v6, /device:TPU:1, one launch (start us, length us, event | category | flops | bytes accessed | tf_op | source)
XLA Modules:
  0.0 145.7 jit_solution(2383695266201007241)
XLA Ops:
  0.0 143.9 %shard_map.28 = bf16[384,512]{1,0:T(8,128)(2,1)} custom-call(bf16[3072,256]{1,0:T(8,128)(2,1)} %bases_ref.1, f32[256,512]{1,0:T(8,128)} %start_ref.1), custom_call_target="tpu_custom_call" | custom-call | tf_op jit(solution)/shard_map/pallas_call | solution.py:588
  143.9 1.8 %copy.4 = bf16[384,512]{1,0:T(8,128)(2,1)} copy(bf16[384,512]{1,0:T(8,128)(2,1)} %shard_map.28) | data formatting | bytes 786432

commit v7 on v6

--- a/solution.py
+++ b/solution.py
@@ -14,6 +14,7 @@
 ORDERS = (("x", "y", "z"), ("y", "z", "x"), ("z", "x", "y")) * 2
 UNITS = (16, 8, 8, 8, 16, 8)
 COLOURS = len(UNITS)
+PARTNER_ORDER = (1, 7, 3, 5, 2, 6, 4)
 HIGHEST = lax.Precision.HIGHEST
 VMEM_SPEC = pl.BlockSpec(memory_space=pltpu.VMEM)
 F32, BF16 = jnp.float32, jnp.bfloat16
@@ -163,7 +164,7 @@
     start_in = [
         [start(turned.at[turned_rows, half * 128:(half + 1) * 128], piece(batch, half), there)
          for half in range(2)]
-        for there in partners
+        for there in (partners[d - 1] for d in PARTNER_ORDER)
     ]
     x_in = [
         start(turned.at[turned_rows, half * 128:(half + 1) * 128], piece(batch, half), there)
@@ -171,8 +172,8 @@
     ]
     block_in = [
         start(bases_ref.at[block_rows((batch + d) % count), :],
-              a_ref.at[own_rows, columns(batch)], there)
-        for d, there in enumerate(partners, 1)
+              a_ref.at[own_rows, columns(batch)], partners[d - 1])
+        for d in PARTNER_ORDER
     ]
     own_block = pltpu.make_async_copy(
         bases_ref.at[block_rows(batch), :], a_ref.at[own_rows, columns(batch)], own_sem.at[2]
@@ -194,7 +195,7 @@
     total = total[:, :128] + total[:, 128:]
 
     energy.begin(total)
-    for distance, pair in enumerate(start_in, 1):
+    for distance, pair in zip(PARTNER_ORDER, start_in):
         for copy in pair:
             copy.wait_recv()
         other = (batch + count - distance) % count
@@ -203,7 +204,7 @@
     for copy in own_start:
         copy.wait()
     own_block.wait()
-    for distance, copy in enumerate(block_in, 1):
+    for distance, copy in zip(PARTNER_ORDER, block_in):
         copy.wait_recv()
         other = (batch + count - distance) % count
         block = a_ref.at[own_rows, columns(other)]
@@ -527,12 +528,13 @@
     over.wait()
     low = jnp.concatenate([side(first, half).astype(BF16) for half in range(2)], axis=0)
     rest[...] = dot_low(low, low, NT)
-    places = [(0, 0), (0, 1), (1, 0), (1, 1), (2, 0), (2, 1), (3, 0), (3, 1)]
-    parts = [(number, range(3 * part, 3 * part + 3)) for number in range(4) for part in range(2)]
+    places = [(0, 0), (0, 1), (1, 0), (1, 1), (2, 0), (2, 1)]
+    parts = [(number, range(3 * part, 3 * part + 3)) for number in range(3) for part in range(2)]
     inverse_factor(
         z_ref, rest, lower, aug, factor_work,
         {place: functools.partial(reduction.step, *part) for place, part in zip(places, parts)},
     )
+    reduction.step(3)
     reduction.join()
 
     def times_factor(value_high, value_low, rows):

time: 146 us -> 144 us (0.986)
  Pallas kernels: 144 us -> 142 us
    pallas_call x1, Pallas kernels: 144 us -> 142 us  [on_device(): pl.pallas_call(whole_kernel, out_shape=jax.ShapeDtypeStruct((height, n),...]
where the time goes in v7:
time: 144 us
  Pallas kernels  142 us (99%)
  local copies, waits for them, and re-layouts  1.77 us (1%)
    pallas_call x1, Pallas kernels, on_device(): pl.pallas_call(whole_kernel, out_shape=jax.ShapeDtypeStruct((height, n),...  142 us

profile of v7, /device:TPU:1, one launch (start us, length us, event | category | flops | bytes accessed | tf_op | source)
XLA Modules:
  0.0 143.7 jit_solution(1189606513196205348)
XLA Ops:
  0.0 141.9 %shard_map.28 = bf16[384,512]{1,0:T(8,128)(2,1)} custom-call(bf16[3072,256]{1,0:T(8,128)(2,1)} %bases_ref.1, f32[256,512]{1,0:T(8,128)} %start_ref.1), custom_call_target="tpu_custom_call" | custom-call | tf_op jit(solution)/shard_map/pallas_call | solution.py:590
  141.9 1.8 %copy.4 = bf16[384,512]{1,0:T(8,128)(2,1)} copy(bf16[384,512]{1,0:T(8,128)(2,1)} %shard_map.28) | data formatting | bytes 786432
